TPU v7x, 32 devices: a whole 2x2x4 slice. The times are simulated.
32 devices in a mesh: dp: 8 (over z, x), tensor: 4 (over y, core).
Axes of the slice: x: 2, y: 2, z: 4, core: 2. Of those that a mesh axis runs over, the one named last changes fastest.
Arguments:
- input_rows: bfloat16 [32768, 768], P(('dp', 'tensor')), may hold values from -6 to 6
- time_embed: bfloat16 [8, 768], P('dp'), may hold values from -4 to 4
- parents: int32 [8, 13], P('dp'), may hold values from 0 to 11, as said below
- qkv_weight: bfloat16 [768, 3, 768], P('dp', None, 'tensor'), may hold values from -0.21875 to 0.21875
- qv_bias: bfloat16 [2, 768], P(None, 'tensor'), may hold values from -0.59765625 to 0.59765625
- out_weight: bfloat16 [768, 768], P('tensor', 'dp'), may hold values from -3.5 to 3.5
- out_bias: bfloat16 [768], replicated, may hold values from -1.796875 to 1.796875
- inner_weight: bfloat16 [768, 3072], P('dp', 'tensor'), may hold values from -0.21875 to 0.21875
- inner_bias: bfloat16 [3072], P('tensor'), may hold values from -1.796875 to 1.796875
- outer_weight: bfloat16 [3072, 768], P('tensor', 'dp'), may hold values from -0.109375 to 0.109375
- outer_bias: bfloat16 [768], replicated, may hold values from -1.796875 to 1.796875
- norm_gain: bfloat16 [2, 768], replicated, may hold values from 0.5 to 1.5
- norm_shift: bfloat16 [2, 768], replicated, may hold values from -1.796875 to 1.796875
- cotangent: bfloat16 [32768, 768], P(('dp', 'tensor')), may hold values from -6 to 6
Outputs:
- block_out: bfloat16 [32768, 768], P(('dp', 'tensor'))
- input_grad: bfloat16 [32768, 768], P(('dp', 'tensor'))
- qkv_weight_grad: float32 [768, 3, 768], P('dp', None, 'tensor')
- qv_bias_grad: float32 [2, 768], P(None, 'tensor')
- out_weight_grad: float32 [768, 768], P('tensor', 'dp')
- out_bias_grad: float32 [768], replicated
- inner_weight_grad: float32 [768, 3072], P('dp', 'tensor')
- inner_bias_grad: float32 [3072], P('tensor')
- outer_weight_grad: float32 [3072, 768], P('tensor', 'dp')
- outer_bias_grad: float32 [768], replicated
- norm_gain_grad: float32 [2, 768], replicated
- norm_shift_grad: float32 [2, 768], replicated
Inputs may be any that keep to these rules, and one draw needn't show every extreme that they name: `parents`: segment 0 is the trunk, positions 0 to 1023 of a tree, and its entry is 0; segment s >= 1 is block 4 + s - 1, and its entry is smaller than s.
All inputs are finite; a program needn't handle non-finite values.
Results may differ from a plain program's by a relative error of at most 0.02.
Values may be sent and summed in bfloat16 or wider, within the bound.
A program may use at most 256 MiB of HBM per device.

v0:
```python
import math

import jax
import jax.numpy as jnp
from jax import lax
from jax.sharding import PartitionSpec as P

D = 768
HEAD_DIM = 64
FF = 3072
TRUNK_BLOCKS = 4
BLOCK = 256
QBLK = 512
SEGS = 13
SEQ = 4096


epsilon = 1e-05
root_half = 0.7071067811865476
inv_root_tau = 0.3989422804014327
far_below = -1e30


def layer_norm(summed, gain_row, shift_row):
    centre = jnp.mean(summed, axis=-1, keepdims=True)
    offset = summed - centre
    inv_std = lax.rsqrt(jnp.mean(offset * offset, axis=-1, keepdims=True) + epsilon)
    normed = offset * inv_std
    return (normed * gain_row + shift_row, normed, inv_std)


def norm_back(grad_out, normed, inv_std, gain_row):
    scaled = grad_out * gain_row
    return inv_std * (
        scaled
        - jnp.mean(scaled, axis=-1, keepdims=True)
        - normed * jnp.mean(scaled * normed, axis=-1, keepdims=True)
    )


def gelu_value(pre_act):
    return 0.5 * pre_act * (1.0 + lax.erf(pre_act * root_half))


def gelu_slope(pre_act):
    return 0.5 * (1.0 + lax.erf(pre_act * root_half)) + pre_act * inv_root_tau * jnp.exp(
        -0.5 * pre_act * pre_act
    )


def block_sight(parent_row):
    seg_ids = jnp.arange(SEGS, dtype=jnp.int32)
    step_up = parent_row[:, None] == seg_ids[None, :]
    identity_mat = seg_ids[:, None] == seg_ids[None, :]
    ancestry = identity_mat
    for repeat_step in range(SEGS):
        reached = jnp.any(jnp.logical_and(step_up[:, :, None], ancestry[None, :, :]), axis=1)
        ancestry = jnp.logical_or(identity_mat, reached)
    block_ids = jnp.arange(SEQ // BLOCK, dtype=jnp.int32)
    segment_of = jnp.maximum(block_ids - TRUNK_BLOCKS + 1, 0)
    row_pick = jnp.take(ancestry, segment_of, axis=0)
    return jnp.take(row_pick, segment_of, axis=1)


def on_device(
    input_rows,
    time_embed,
    parents,
    qkv_weight,
    qv_bias,
    out_weight,
    out_bias,
    inner_weight,
    inner_bias,
    outer_weight,
    outer_bias,
    norm_gain,
    norm_shift,
    cotangent,
):
    tensor_rank = lax.axis_index("tensor")
    scale_factor = 1.0 / math.sqrt(HEAD_DIM)
    span_count = QBLK // BLOCK
    query_blocks = SEQ // QBLK
    qkv_all, out_all = (
        lax.all_gather(qkv_weight, "dp", axis=0, tiled=True),
        lax.all_gather(out_weight, "dp", axis=1, tiled=True),
    )
    inner_all, outer_all = (
        lax.all_gather(inner_weight, "dp", axis=0, tiled=True),
        lax.all_gather(outer_weight, "dp", axis=1, tiled=True),
    )
    quarter = qkv_all.shape[2]
    heads_here = quarter // HEAD_DIM
    gain_rows = norm_gain.astype(jnp.float32)
    shift_rows = norm_shift.astype(jnp.float32)
    start_sum = input_rows.astype(jnp.float32) + time_embed.astype(jnp.float32)
    start_low = start_sum.astype(jnp.bfloat16)
    whole_start = lax.all_gather(start_low, "tensor", axis=0, tiled=True)
    projected = jnp.einsum("td,dcf->tcf", whole_start, qkv_all, preferred_element_type=jnp.float32)
    bias_pair = qv_bias.astype(jnp.float32)
    queries = (
        (projected[:, 0] + bias_pair[0]).astype(jnp.bfloat16).reshape(SEQ, heads_here, HEAD_DIM)
    )
    key_rows = projected[:, 1].astype(jnp.bfloat16).reshape(SEQ, heads_here, HEAD_DIM)
    value_rows = (
        (projected[:, 2] + bias_pair[1]).astype(jnp.bfloat16).reshape(SEQ, heads_here, HEAD_DIM)
    )
    sight_map = block_sight(parents[0])

    def masked_scores(block_index):
        query_block = lax.dynamic_slice_in_dim(queries, block_index * QBLK, QBLK, 0)
        sight_rows = lax.dynamic_slice_in_dim(sight_map, block_index * span_count, span_count, 0)
        seen_mask = jnp.repeat(jnp.repeat(sight_rows, BLOCK, axis=0), BLOCK, axis=1)
        raw_scores = (
            jnp.einsum("qhd,khd->hqk", query_block, key_rows, preferred_element_type=jnp.float32)
            * scale_factor
        )
        return (jnp.where(seen_mask[None], raw_scores, far_below), query_block)

    def attend(block_index):
        scores, query_block = masked_scores(block_index)
        row_max = jnp.max(scores, axis=-1, keepdims=True)
        exp_terms = jnp.exp(scores - row_max)
        row_total = jnp.sum(exp_terms, axis=-1, keepdims=True)
        probs_low = (exp_terms / row_total).astype(jnp.bfloat16)
        mixed_block = jnp.einsum(
            "hqk,khd->qhd", probs_low, value_rows, preferred_element_type=jnp.float32
        )
        return (mixed_block.astype(jnp.bfloat16), (row_max + jnp.log(row_total))[..., 0])

    block_ids = jnp.arange(query_blocks, dtype=jnp.int32)
    mixed_blocks, log_totals = lax.map(attend, block_ids)
    mixed_heads = mixed_blocks.reshape(SEQ, quarter)
    attn_out = lax.psum_scatter(
        jnp.dot(mixed_heads, out_all, preferred_element_type=jnp.float32).astype(jnp.bfloat16),
        "tensor",
        scatter_dimension=0,
        tiled=True,
    ).astype(jnp.float32) + out_bias.astype(jnp.float32)
    hidden, normed_first, inv_std_first = layer_norm(
        start_sum + attn_out, gain_rows[0], shift_rows[0]
    )
    hidden_low = hidden.astype(jnp.bfloat16)
    whole_hidden = lax.all_gather(hidden_low, "tensor", axis=0, tiled=True)
    pre_act = jnp.dot(
        whole_hidden, inner_all, preferred_element_type=jnp.float32
    ) + inner_bias.astype(jnp.float32)
    act_low = gelu_value(pre_act).astype(jnp.bfloat16)
    mlp_out = lax.psum_scatter(
        jnp.dot(act_low, outer_all, preferred_element_type=jnp.float32).astype(jnp.bfloat16),
        "tensor",
        scatter_dimension=0,
        tiled=True,
    ).astype(jnp.float32)
    final_rows, normed_second, inv_std_second = layer_norm(
        hidden + mlp_out + outer_bias.astype(jnp.float32), gain_rows[1], shift_rows[1]
    )
    block_out = final_rows.astype(jnp.bfloat16)
    grad_final = cotangent.astype(jnp.float32)
    gain_grad_second = jnp.sum(grad_final * normed_second, axis=0)
    shift_grad_second = jnp.sum(grad_final, axis=0)
    grad_second = norm_back(grad_final, normed_second, inv_std_second, gain_rows[1])
    grad_m_low = grad_second.astype(jnp.bfloat16)
    outer_bias_part = jnp.sum(grad_m_low, axis=0, dtype=jnp.float32)
    whole_grad_m = lax.all_gather(grad_m_low, "tensor", axis=0, tiled=True)
    outer_grad = jnp.einsum("tf,td->fd", act_low, whole_grad_m, preferred_element_type=jnp.float32)
    grad_act = jnp.einsum("td,fd->tf", whole_grad_m, outer_all, preferred_element_type=jnp.float32)
    grad_pre = (grad_act * gelu_slope(pre_act)).astype(jnp.bfloat16)
    inner_bias_part = jnp.sum(grad_pre, axis=0, dtype=jnp.float32)
    inner_bias_full = lax.dynamic_update_slice_in_dim(
        jnp.zeros((FF,), jnp.float32), inner_bias_part, tensor_rank * inner_bias_part.shape[0], 0
    )
    inner_grad = jnp.einsum("td,tf->df", whole_hidden, grad_pre, preferred_element_type=jnp.float32)
    grad_hidden = lax.psum_scatter(
        jnp.einsum("tf,df->td", grad_pre, inner_all, preferred_element_type=jnp.float32).astype(
            jnp.bfloat16
        ),
        "tensor",
        scatter_dimension=0,
        tiled=True,
    ).astype(jnp.float32)
    grad_first_in = grad_hidden + grad_second
    gain_grad_first = jnp.sum(grad_first_in * normed_first, axis=0)
    shift_grad_first = jnp.sum(grad_first_in, axis=0)
    grad_first = norm_back(grad_first_in, normed_first, inv_std_first, gain_rows[0])
    grad_a_low = grad_first.astype(jnp.bfloat16)
    out_bias_part = jnp.sum(grad_a_low, axis=0, dtype=jnp.float32)
    whole_grad_a = lax.all_gather(grad_a_low, "tensor", axis=0, tiled=True)
    out_grad = jnp.einsum(
        "tc,td->cd", mixed_heads, whole_grad_a, preferred_element_type=jnp.float32
    )
    grad_mixed = (
        jnp.einsum("td,cd->tc", whole_grad_a, out_all, preferred_element_type=jnp.float32)
        .astype(jnp.bfloat16)
        .reshape(SEQ, heads_here, HEAD_DIM)
    )

    def attend_back(running, pieces):
        key_sum, value_sum = running
        block_index, log_total = pieces
        scores, query_block = masked_scores(block_index)
        attn_probs = jnp.exp(scores - log_total[..., None])
        grad_block = lax.dynamic_slice_in_dim(grad_mixed, block_index * QBLK, QBLK, 0)
        grad_probs = jnp.einsum(
            "qhd,khd->hqk", grad_block, value_rows, preferred_element_type=jnp.float32
        )
        centre = jnp.sum(attn_probs * grad_probs, axis=-1, keepdims=True)
        grad_scores = (attn_probs * (grad_probs - centre)).astype(jnp.bfloat16)
        query_grad = (
            jnp.einsum("hqk,khd->qhd", grad_scores, key_rows, preferred_element_type=jnp.float32)
            * scale_factor
        ).astype(jnp.bfloat16)
        key_sum = (
            key_sum
            + jnp.einsum(
                "hqk,qhd->khd", grad_scores, query_block, preferred_element_type=jnp.float32
            )
            * scale_factor
        )
        value_sum = value_sum + jnp.einsum(
            "hqk,qhd->khd",
            attn_probs.astype(jnp.bfloat16),
            grad_block,
            preferred_element_type=jnp.float32,
        )
        return ((key_sum, value_sum), query_grad)

    zero_rows = jnp.zeros((SEQ, heads_here, HEAD_DIM), jnp.float32)
    (key_sum, value_sum), query_grads = lax.scan(
        attend_back, (zero_rows, zero_rows), (block_ids, log_totals)
    )
    query_grad = query_grads.reshape(SEQ, quarter)
    key_grad = key_sum.astype(jnp.bfloat16).reshape(SEQ, quarter)
    value_grad = value_sum.astype(jnp.bfloat16).reshape(SEQ, quarter)
    grad_proj = jnp.stack([query_grad, key_grad, value_grad], axis=1)
    qkv_grad = jnp.einsum("td,tcf->dcf", whole_start, grad_proj, preferred_element_type=jnp.float32)
    grad_start = lax.psum_scatter(
        jnp.einsum("tcf,dcf->td", grad_proj, qkv_all, preferred_element_type=jnp.float32).astype(
            jnp.bfloat16
        ),
        "tensor",
        scatter_dimension=0,
        tiled=True,
    ).astype(jnp.float32)
    input_grad = (grad_start + grad_first).astype(jnp.bfloat16)
    qkv_share, out_share, inner_share, outer_share = (
        lax.psum_scatter(qkv_grad, "dp", scatter_dimension=0, tiled=True),
        lax.psum_scatter(out_grad, "dp", scatter_dimension=1, tiled=True),
        lax.psum_scatter(inner_grad, "dp", scatter_dimension=0, tiled=True),
        lax.psum_scatter(outer_grad, "dp", scatter_dimension=1, tiled=True),
    )
    pair_part = jnp.stack(
        [
            jnp.sum(query_grad, axis=0, dtype=jnp.float32),
            jnp.sum(value_grad, axis=0, dtype=jnp.float32),
        ]
    )
    pair_full = lax.dynamic_update_slice_in_dim(
        jnp.zeros((2, D), jnp.float32), pair_part, tensor_rank * quarter, 1
    )
    small_sums = lax.psum(
        (
            pair_full,
            out_bias_part,
            inner_bias_full,
            outer_bias_part,
            jnp.stack([gain_grad_first, gain_grad_second]),
            jnp.stack([shift_grad_first, shift_grad_second]),
        ),
        ("dp", "tensor"),
    )
    hidden_share = FF // lax.axis_size("tensor")
    qv_bias_grad = lax.dynamic_slice_in_dim(small_sums[0], tensor_rank * quarter, quarter, 1)
    inner_bias_grad = lax.dynamic_slice_in_dim(
        small_sums[2], tensor_rank * hidden_share, hidden_share, 0
    )
    return (
        block_out,
        input_grad,
        qkv_share,
        qv_bias_grad,
        out_share,
        small_sums[1],
        inner_share,
        inner_bias_grad,
        outer_share,
        small_sums[3],
        small_sums[4],
        small_sums[5],
    )


def solution(mesh):
    return jax.shard_map(
        on_device,
        mesh=mesh,
        in_specs=(
            P(("dp", "tensor"), None),
            P("dp", None),
            P("dp", None),
            P("dp", None, "tensor"),
            P(None, "tensor"),
            P("tensor", "dp"),
            P(),
            P("dp", "tensor"),
            P("tensor"),
            P("tensor", "dp"),
            P(),
            P(),
            P(),
            P(("dp", "tensor"), None),
        ),
        out_specs=(
            P(("dp", "tensor"), None),
            P(("dp", "tensor"), None),
            P("dp", None, "tensor"),
            P(None, "tensor"),
            P("tensor", "dp"),
            P(),
            P("dp", "tensor"),
            P("tensor"),
            P("tensor", "dp"),
            P(),
            P(),
            P(),
        ),
        check_vma=False,
    )
```

profile of v0, /device:TPU:0, one launch (start us, length us, event | category | flops | bytes accessed | tf_op | source)
XLA Modules:
  0.0 1948.6 jit_solution(3673868844371814140)
XLA Ops:
  16.1 38.7 %all_gather.25 = bf16[768,3,192]{2,1,0:T(4,128)(2,1)S(1)} all-gather(bf16[96,3,192]{2,1,0:T(4,128)(2,1)S(1)} %copy.52), channel_id=1, replica_groups=mesh['dp'=8,'tensor'=4] {'dp'}, dimensions={0}, use_global_device_ids=true | all-gather | bytes 995328 | tf_op jit(solution)/shard_map/all_gather | solution.py:86
  55.7 33.2 %all_gather.26 = bf16[192,768]{0,1:T(8,128)(2,1)} all-gather(bf16[192,96]{0,1:T(8,128)(2,1)S(1)} %copy.56), channel_id=1, replica_groups=mesh['dp'=8,'tensor'=4] {'dp'}, dimensions={1}, use_global_device_ids=true | all-gather | bytes 331776 | tf_op jit(solution)/shard_map/all_gather | solution.py:87
  99.2 355.9 %while.27 = (s32[]{:T(128)}, bf16[8,512,3,64]{1,3,2,0:T(8,128)(2,1)}, f32[8,3,512]{2,1,0:T(4,128)}, s32[8]{0:T(128)S(1)}, pred[16,16]{1,0:T(8,128)(4,1)S(1)}, /*...) while((s32[]{:T(128)}, ...), condition=%wide.region_16.17_spmd, body=%wide.region_13.16_spmd.sunk | while | flops 1686206976 | bytes 91687272 | solution.py:133
  467.5 56.1 %reduce-scatter.11.cloned.1.call-done = bf16[1024,768]{1,0:T(8,128)(2,1)} async-done(((bf16[4096,768]{1,0:T(8,128)(2,1)}), bf16[1024,768]{1,0:T(8,128)(2,1)}) %reduce-scatter.11.cloned.1.call-update) | async-done | bytes 1572880 | tf_op jit(solution)/shard_map/reduce_scatter | solution.py:135
  531.5 44.4 %all-gather.9.cloned.1.call-done = bf16[4096,768]{1,0:T(8,128)(2,1)} async-done(((bf16[1024,768]{1,0:T(8,128)(2,1)}), bf16[4096,768]{1,0:T(8,128)(2,1)}) %all-gather.9.cloned.1.call-update) | async-done | bytes 6291472 | tf_op jit(solution)/shard_map/all_gather | solution.py:145
  588.1 31.7 %all-gather.13.cloned.1.call-done = bf16[768,768]{0,1:T(8,128)(2,1)} async-done(((bf16[768,96]{0,1:T(8,128)(2,1)}), bf16[768,768]{0,1:T(8,128)(2,1)}) %all-gather.13.cloned.1.call-update) | async-done | bytes 1179664 | tf_op jit(solution)/shard_map/all_gather | solution.py:91
  630.3 55.5 %reduce-scatter.13.cloned.1.call-done = bf16[1024,768]{1,0:T(8,128)(2,1)} async-done(((bf16[4096,768]{1,0:T(8,128)(2,1)}), bf16[1024,768]{1,0:T(8,128)(2,1)}) %reduce-scatter.13.cloned.1.call-update) | async-done | bytes 1572880 | tf_op jit(solution)/shard_map/reduce_scatter | solution.py:150
  697.0 46.5 %all-gather.15.cloned.1.call-done = bf16[4096,768]{1,0:T(8,128)(2,1)} async-done(((bf16[1024,768]{1,0:T(8,128)(2,1)}), bf16[4096,768]{1,0:T(8,128)(2,1)}) %all-gather.15.cloned.1.call-update) | async-done | bytes 6291472 | tf_op jit(solution)/shard_map/all_gather | solution.py:166
  743.5 12.8 convert_reduce_fusion
  766.2 58.3 %reduce-scatter.15.cloned.1.call-done = bf16[1024,768]{1,0:T(8,128)(2,1)} async-done(((bf16[4096,768]{1,0:T(8,128)(2,1)}), bf16[1024,768]{1,0:T(8,128)(2,1)}) %reduce-scatter.15.cloned.1.call-update) | async-done | bytes 1572880 | tf_op jit(solution)/shard_map/reduce_scatter | solution.py:175
  833.2 46.5 %all-gather.17.cloned.1.call-done = bf16[4096,768]{1,0:T(8,128)(2,1)} async-done(((bf16[1024,768]{1,0:T(8,128)(2,1)}), bf16[4096,768]{1,0:T(8,128)(2,1)}) %all-gather.17.cloned.1.call-update) | async-done | bytes 6291472 | tf_op jit(solution)/shard_map/all_gather | solution.py:189
  893.9 752.9 %while.28 = (s32[]{:T(128)}, f32[4096,3,64]{0,2,1:T(8,128)}, f32[4096,3,64]{0,2,1:T(8,128)}, bf16[8,512,3,64]{1,3,2,0:T(8,128)(2,1)}, s32[8]{0:T(128)S(1)}, /*in...) while((s32[]{:T(128)}, f32[4096,3,64]{0,2,1:T(8,128)}, ...), condition=%wide.region_30.31_spmd.clone, body=%wide.region_28.30_spmd.clone.sunk | while | flops 4125030912 | bytes 244836784 | solution.py:230
  902.7 13.4 fusion.137
  916.1 13.0 fusion.139
  929.2 18.2 multiply_reduce_fusion.7
  947.3 21.7 %multiply_convert_fusion.3 = bf16[3,512,4096]{2,1,0:T(8,128)(2,1)} fusion(f32[3,512,4096]{2,1,0:T(8,128)} %get-tuple-element.436, f32[3,512,4096]{2,1,0:T(8,128)} %fusion.137, f32[3,512]{1,0:T(4,128)S(1)} %get-tuple-element.437, f32[3,512]{1,0:T(4,128)S(1)} %dynamic-slice_bitcast_fusion.2, pred[512,4096]{1,0:T(8,128)(4,1)S(1)} %bitcast.140), kind=kLoop, calls=%fused_computation.18.clone.1 | loop fusion | flops 37748736 | bytes 65024000 | tf_op jit(solution)/shard_map/while/body/eval_jaxpr/convert_element_type | solution.py:209
  996.2 13.3 fusion.137
  1009.5 13.8 fusion.139
  1023.3 18.2 multiply_reduce_fusion.7
  1041.5 21.7 %multiply_convert_fusion.3 = bf16[3,512,4096]{2,1,0:T(8,128)(2,1)} fusion(f32[3,512,4096]{2,1,0:T(8,128)} %get-tuple-element.436, f32[3,512,4096]{2,1,0:T(8,128)} %fusion.137, f32[3,512]{1,0:T(4,128)S(1)} %get-tuple-element.437, f32[3,512]{1,0:T(4,128)S(1)} %dynamic-slice_bitcast_fusion.2, pred[512,4096]{1,0:T(8,128)(4,1)S(1)} %bitcast.140), kind=kLoop, calls=%fused_computation.18.clone.1 | loop fusion | flops 37748736 | bytes 65024000 | tf_op jit(solution)/shard_map/while/body/eval_jaxpr/convert_element_type | solution.py:209
  1090.3 13.3 fusion.137
  1103.6 13.8 fusion.139
  1117.4 18.2 multiply_reduce_fusion.7
  1135.6 21.7 %multiply_convert_fusion.3 = bf16[3,512,4096]{2,1,0:T(8,128)(2,1)} fusion(f32[3,512,4096]{2,1,0:T(8,128)} %get-tuple-element.436, f32[3,512,4096]{2,1,0:T(8,128)} %fusion.137, f32[3,512]{1,0:T(4,128)S(1)} %get-tuple-element.437, f32[3,512]{1,0:T(4,128)S(1)} %dynamic-slice_bitcast_fusion.2, pred[512,4096]{1,0:T(8,128)(4,1)S(1)} %bitcast.140), kind=kLoop, calls=%fused_computation.18.clone.1 | loop fusion | flops 37748736 | bytes 65024000 | tf_op jit(solution)/shard_map/while/body/eval_jaxpr/convert_element_type | solution.py:209
  1184.4 13.3 fusion.137
  1197.7 13.8 fusion.139
  1211.5 18.2 multiply_reduce_fusion.7
  1229.7 21.7 %multiply_convert_fusion.3 = bf16[3,512,4096]{2,1,0:T(8,128)(2,1)} fusion(f32[3,512,4096]{2,1,0:T(8,128)} %get-tuple-element.436, f32[3,512,4096]{2,1,0:T(8,128)} %fusion.137, f32[3,512]{1,0:T(4,128)S(1)} %get-tuple-element.437, f32[3,512]{1,0:T(4,128)S(1)} %dynamic-slice_bitcast_fusion.2, pred[512,4096]{1,0:T(8,128)(4,1)S(1)} %bitcast.140), kind=kLoop, calls=%fused_computation.18.clone.1 | loop fusion | flops 37748736 | bytes 65024000 | tf_op jit(solution)/shard_map/while/body/eval_jaxpr/convert_element_type | solution.py:209
  1278.5 13.3 fusion.137
  1291.8 13.8 fusion.139
  1305.6 18.2 multiply_reduce_fusion.7
  1323.8 21.7 %multiply_convert_fusion.3 = bf16[3,512,4096]{2,1,0:T(8,128)(2,1)} fusion(f32[3,512,4096]{2,1,0:T(8,128)} %get-tuple-element.436, f32[3,512,4096]{2,1,0:T(8,128)} %fusion.137, f32[3,512]{1,0:T(4,128)S(1)} %get-tuple-element.437, f32[3,512]{1,0:T(4,128)S(1)} %dynamic-slice_bitcast_fusion.2, pred[512,4096]{1,0:T(8,128)(4,1)S(1)} %bitcast.140), kind=kLoop, calls=%fused_computation.18.clone.1 | loop fusion | flops 37748736 | bytes 65024000 | tf_op jit(solution)/shard_map/while/body/eval_jaxpr/convert_element_type | solution.py:209
  1372.6 13.3 fusion.137
  1385.9 13.8 fusion.139
  1399.8 18.2 multiply_reduce_fusion.7
  1417.9 21.7 %multiply_convert_fusion.3 = bf16[3,512,4096]{2,1,0:T(8,128)(2,1)} fusion(f32[3,512,4096]{2,1,0:T(8,128)} %get-tuple-element.436, f32[3,512,4096]{2,1,0:T(8,128)} %fusion.137, f32[3,512]{1,0:T(4,128)S(1)} %get-tuple-element.437, f32[3,512]{1,0:T(4,128)S(1)} %dynamic-slice_bitcast_fusion.2, pred[512,4096]{1,0:T(8,128)(4,1)S(1)} %bitcast.140), kind=kLoop, calls=%fused_computation.18.clone.1 | loop fusion | flops 37748736 | bytes 65024000 | tf_op jit(solution)/shard_map/while/body/eval_jaxpr/convert_element_type | solution.py:209
  1466.8 13.3 fusion.137
  1480.0 13.8 fusion.139
  1493.9 18.2 multiply_reduce_fusion.7
  1512.1 21.7 %multiply_convert_fusion.3 = bf16[3,512,4096]{2,1,0:T(8,128)(2,1)} fusion(f32[3,512,4096]{2,1,0:T(8,128)} %get-tuple-element.436, f32[3,512,4096]{2,1,0:T(8,128)} %fusion.137, f32[3,512]{1,0:T(4,128)S(1)} %get-tuple-element.437, f32[3,512]{1,0:T(4,128)S(1)} %dynamic-slice_bitcast_fusion.2, pred[512,4096]{1,0:T(8,128)(4,1)S(1)} %bitcast.140), kind=kLoop, calls=%fused_computation.18.clone.1 | loop fusion | flops 37748736 | bytes 65024000 | tf_op jit(solution)/shard_map/while/body/eval_jaxpr/convert_element_type | solution.py:209
  1560.9 13.3 fusion.137
  1574.2 13.8 fusion.139
  1588.0 18.2 multiply_reduce_fusion.7
  1606.2 21.7 %multiply_convert_fusion.3 = bf16[3,512,4096]{2,1,0:T(8,128)(2,1)} fusion(f32[3,512,4096]{2,1,0:T(8,128)} %get-tuple-element.436, f32[3,512,4096]{2,1,0:T(8,128)} %fusion.137, f32[3,512]{1,0:T(4,128)S(1)} %get-tuple-element.437, f32[3,512]{1,0:T(4,128)S(1)} %dynamic-slice_bitcast_fusion.2, pred[512,4096]{1,0:T(8,128)(4,1)S(1)} %bitcast.140), kind=kLoop, calls=%fused_computation.18.clone.1 | loop fusion | flops 37748736 | bytes 65024000 | tf_op jit(solution)/shard_map/while/body/eval_jaxpr/convert_element_type | solution.py:209
  1696.9 41.9 %all-reduce = (f32[2,768]{1,0:T(2,128)S(1)}, f32[768]{0:T(1024)}, f32[3072]{0:T(1024)S(1)}, f32[768]{0:T(1024)}, f32[2,768]{1,0:T(2,128)}, /*index=5*/f32[2,768]{1,0:T(2,128)}) all-reduce(f32[2,768]{1,0:T(2,128)S(1)} %dynamic_update_slice.17, f32[768]{0:T(1024)S(1)} %copy-done.28, ...), channel_id=1, replica_groups=mesh['dp'=8,'tensor'=4] {'dp','tensor'}, use_global_device_ids=true, to_apply=%region_35.36 | all-reduce | flops 9216 | bytes 73728 | tf_op jit(solution)/shard_map/psum | solution.py:262
  1745.7 50.8 %reduce-scatter.21.cloned.1.call-done = f32[96,768]{1,0:T(8,128)} async-done(((f32[768,768]{1,0:T(8,128)}), f32[96,768]{1,0:T(8,128)}) %reduce-scatter.21.cloned.1.call-update) | async-done | bytes 294928 | tf_op jit(solution)/shard_map/reduce_scatter | solution.py:250
  1796.4 72.4 %reduce-scatter.23.cloned.1.call-done = f32[768,96]{0,1:T(8,128)} async-done(((f32[768,768]{0,1:T(8,128)}), f32[768,96]{0,1:T(8,128)}) %reduce-scatter.23.cloned.1.call-update) | async-done | bytes 294928 | tf_op jit(solution)/shard_map/reduce_scatter | solution.py:251
  1868.8 72.5 %reduce-scatter.19.cloned.1.call-done = f32[96,3,192]{2,0,1:T(8,128)} async-done(((f32[768,3,192]{2,0,1:T(8,128)}), f32[96,3,192]{2,0,1:T(8,128)}) %reduce-scatter.19.cloned.1.call-update) | async-done | bytes 221200 | tf_op jit(solution)/shard_map/reduce_scatter | solution.py:248
  (392 shorter events, 712.9 us)
Async XLA Ops:
  8.0 4.3 copy-start.37
  8.0 4.6 copy-start.38
  8.0 7.9 copy-start.22
  8.0 8.0 copy-start.19
  8.1 80.9 %all-gather.7.cloned.1.call-start = ((), (), s32[]{:S(2)}) async-start(), calls=%async_computation.8 | async-start | bytes 7864320 | tf_op jit(solution)/shard_map/all_gather | solution.py:99
  12.3 511.4 %reduce-scatter.11.cloned.1.call-start = ((), (), s32[]{:S(2)}) async-start(), calls=%async_computation.9 | async-start | bytes 7864320 | tf_op jit(solution)/shard_map/reduce_scatter | solution.py:135
  55.7 39.2 %copy-start.15 = (bf16[768,3,192]{0,2,1:T(8,128)(2,1)}, bf16[768,3,192]{0,2,1:T(8,128)(2,1)S(1)}, u32[]{:S(2)}) copy-start(bf16[768,3,192]{0,2,1:T(8,128)(2,1)S(1)} %copy.53) | copy-start | bytes 2654212
  455.7 4.1 copy-start.4
  455.7 4.1 copy-start.8
  455.7 5.3 copy-start.11
  465.5 58.1 %copy-start.2 = (bf16[1024,768]{1,0:T(8,128)(2,1)S(1)}, bf16[1024,768]{1,0:T(8,128)(2,1)}, u32[]{:S(2)}) copy-start(bf16[1024,768]{1,0:T(8,128)(2,1)} %param.18) | copy-start | bytes 4718596
  465.5 58.1 %copy-start.18 = (f32[768]{0:T(1024)S(1)}, f32[768]{0:T(1024)}, u32[]{:S(2)}) copy-start(f32[768]{0:T(1024)} %copy-done.17) | copy-start | bytes 9220
  465.6 65.9 %all-gather.11.cloned.1.call-start = ((), (), s32[]{:S(2)}) async-start(), calls=%async_computation.11 | async-start | bytes 1327104 | tf_op jit(solution)/shard_map/all_gather | solution.py:90
  466.2 109.8 %all-gather.9.cloned.1.call-start = ((), (), s32[]{:S(2)}) async-start(), calls=%async_computation.10 | async-start | bytes 7864320 | tf_op jit(solution)/shard_map/all_gather | solution.py:145
  523.7 3.8 copy-start.23
  529.6 90.2 %all-gather.13.cloned.1.call-start = ((), (), s32[]{:S(2)}) async-start(), calls=%async_computation.12 | async-start | bytes 1327104 | tf_op jit(solution)/shard_map/all_gather | solution.py:91
  530.2 155.7 %reduce-scatter.13.cloned.1.call-start = ((), (), s32[]{:S(2)}) async-start(), calls=%async_computation.13 | async-start | bytes 7864320 | tf_op jit(solution)/shard_map/reduce_scatter | solution.py:150
  629.0 114.5 %all-gather.15.cloned.1.call-start = ((), (), s32[]{:S(2)}) async-start(), calls=%async_computation.14 | async-start | bytes 7864320 | tf_op jit(solution)/shard_map/all_gather | solution.py:166
  689.7 3.2 copy-start.29
  696.9 127.5 %reduce-scatter.15.cloned.1.call-start = ((), (), s32[]{:S(2)}) async-start(), calls=%async_computation.15 | async-start | bytes 7864320 | tf_op jit(solution)/shard_map/reduce_scatter | solution.py:175
  743.5 15.4 copy-start.39
  756.3 2.6 copy-start.40
  766.1 113.5 %all-gather.17.cloned.1.call-start = ((), (), s32[]{:S(2)}) async-start(), calls=%async_computation.16 | async-start | bytes 7864320 | tf_op jit(solution)/shard_map/all_gather | solution.py:189
  824.4 4.8 copy-start.5
  824.5 4.8 copy-start.9
  824.5 4.8 copy-start.21
  833.1 907.0 %reduce-scatter.25.cloned.1.call-start = ((), (), s32[]{:S(2)}) async-start(), calls=%async_computation.21 | async-start | bytes 884736
  886.4 855.4 %reduce-scatter.17.cloned.1.call-start = ((), (), s32[]{:S(2)}) async-start(), calls=%async_computation.17 | async-start | bytes 7864320 | tf_op jit(solution)/shard_map/reduce_scatter | solution.py:238
  969.1 9.8 copy-start
  1063.2 9.8 copy-start
  1157.3 9.8 copy-start
  1251.4 9.8 copy-start
  1345.5 9.8 copy-start
  1439.7 9.8 copy-start
  1533.8 9.8 copy-start
  1627.9 9.8 copy-start
  1646.7 3.4 copy-start.6
  1653.1 3.6 copy-start.12
  1653.1 3.6 copy-start.13
  1653.1 3.6 copy-start.16
  1663.8 132.6 %reduce-scatter.21.cloned.1.call-start = ((), (), s32[]{:S(2)}) async-start(), calls=%async_computation.19 | async-start | bytes 2654208 | tf_op jit(solution)/shard_map/reduce_scatter | solution.py:250
  1674.2 194.6 %reduce-scatter.23.cloned.1.call-start = ((), (), s32[]{:S(2)}) async-start(), calls=%async_computation.20 | async-start | bytes 2654208 | tf_op jit(solution)/shard_map/reduce_scatter | solution.py:251
  1684.9 10.9 copy-start.31
  1684.9 10.9 copy-start.30
  1685.0 10.9 copy-start.32
  1685.0 11.2 copy-start.26
  1685.0 11.2 copy-start.25
  1685.0 256.3 %reduce-scatter.19.cloned.1.call-start = ((), (), s32[]{:S(2)}) async-start(), calls=%async_computation.18 | async-start | bytes 2654208 | tf_op jit(solution)/shard_map/reduce_scatter | solution.py:248
  (21 other events, 26.6 us)
Sparse Core Ops, SparseCore 0:
  12.4 49.0 all-gather.6
  465.7 57.8 reduce-scatter.10
  697.1 46.3 all-gather.14
  833.2 46.3 all-gather.16
Sparse Core Ops, SparseCore 1:
  468.2 40.8 all-gather.10
  529.7 46.2 all-gather.8
  578.3 41.5 all-gather.12
  629.1 56.7 reduce-scatter.12
  766.2 58.2 reduce-scatter.14
  886.4 62.5 reduce-scatter.24
  1663.9 58.9 reduce-scatter.16
  1727.2 69.2 reduce-scatter.20
  1800.8 68.0 reduce-scatter.22
  1873.3 67.9 reduce-scatter.18
where the time goes:
time: 1960 us; the launch traced here: 1950 us
  matrix products  801 us (41%)
  waiting for transfers between devices  536 us (27%)
  other arithmetic  316 us (16%)
  local copies, waits for them, and re-layouts  142 us (7%)
  blocking collectives  114 us (6%)
  loops' own time  22.8 us (1%)
    dot_general x16, matrix products, masked_scores(): jnp.einsum('qhd,khd->hqk', query_block, key_rows, preferred_element_type=...  205 us
    convert_element_type x8, other arithmetic, attend_back(): grad_scores = (attn_probs * (grad_probs - centre)).astype(jnp.bfloat16)  174 us
    dot_general x8, matrix products, attend_back(): jnp.einsum('qhd,khd->hqk', grad_block, value_rows, preferred_element_type...  145 us
    dot_general x8, matrix products, attend_back(): jnp.einsum('hqk,qhd->khd', attn_probs.astype(jnp.bfloat16), grad_block, p...  110 us
    dot_general x8, matrix products, attend(): jnp.einsum('hqk,khd->qhd', probs_low, value_rows, preferred_element_type=...  101 us
    reduce_sum x8, other arithmetic, attend(): row_total = jnp.sum(exp_terms, axis=-1, keepdims=True)  94.6 us
    dot_general x8, matrix products, attend_back(): jnp.einsum('hqk,khd->qhd', grad_scores, key_rows, preferred_element_type=...  78 us
    reduce_scatter x1, waiting for transfers between devices, on_device(): lax.psum_scatter(qkv_grad, 'dp', scatter_dimension=0, tiled=True)  72.5 us
  transfers between devices with their start and end apart: 14, of which 10 were waited for; matrix products, arithmetic and copies ran while one was open for 42% of the time, Pallas kernels for 0%

commit v1 on v0

v1 whole, which is shorter than its diff:
```python
import functools
import math

import jax
import jax.numpy as jnp
from jax import lax
from jax.experimental import pallas as pl
from jax.experimental.pallas import tpu as pltpu
from jax.sharding import PartitionSpec as P

bf=jnp.bfloat16; f32=jnp.float32
LOG2E=1.4426950408889634
BLK=256; TRUNK=1024; NB=16; HD=64; HN=3

def _masked(t, h):
    z=jnp.zeros((HD,t.shape[1]),t.dtype)
    if h==0: return jnp.concatenate([t,z],0)
    if h==1: return jnp.concatenate([z,t],0)
    return t
def _lanes(h): return slice(0,128) if h<2 else slice(128,192)

def fwd_kernel(path_ref, cnt_ref, qt_ref, k_ref, vt_ref, o_ref, lse_ref, m_s, acc_s):
    def qblock(i, _):
        qs=pl.ds(pl.multiple_of(i*BLK,BLK),BLK)
        qm=[_masked(qt_ref[h*HD:(h+1)*HD,qs],h) for h in range(HN)]
        for h in range(HN):
            s=jnp.dot(k_ref[0:TRUNK,_lanes(h)],qm[h],preferred_element_type=f32)*LOG2E
            m=jnp.max(s,axis=0,keepdims=True)
            p=jnp.exp2(s-m).astype(bf)
            acc_s[h]=jnp.dot(vt_ref[h,:,0:TRUNK],p,preferred_element_type=f32)
            m_s[h:h+1]=m
        def step(j,_):
            kb=path_ref[i,j]
            ks=pl.ds(pl.multiple_of(kb*BLK,BLK),BLK)
            for h in range(HN):
                s=jnp.dot(k_ref[ks,_lanes(h)],qm[h],preferred_element_type=f32)*LOG2E
                mo=m_s[h:h+1]
                m=jnp.maximum(mo,jnp.max(s,axis=0,keepdims=True))
                al=jnp.exp2(mo-m)
                p=jnp.exp2(s-m).astype(bf)
                acc_s[h]=acc_s[h]*al+jnp.dot(vt_ref[h,:,ks],p,preferred_element_type=f32)
                m_s[h:h+1]=m
            return 0
        lax.fori_loop(0,cnt_ref[i],step,0)
        for h in range(HN):
            l=acc_s[h,HD:HD+1,:]
            o_ref[h*HD:(h+1)*HD,qs]=acc_s[h,0:HD,:]/l
            lse_ref[h:h+1,qs]=m_s[h:h+1]+jnp.log2(l)
        return 0
    lax.fori_loop(0,NB,qblock,0)

def attn_fwd(path,cnt,qt,k,vt):
    S=qt.shape[1]
    vm=pl.BlockSpec(memory_space=pltpu.VMEM); sm=pl.BlockSpec(memory_space=pltpu.SMEM)
    return pl.pallas_call(fwd_kernel,
        out_shape=(jax.ShapeDtypeStruct((HN*HD,S),f32),jax.ShapeDtypeStruct((8,S),f32)),
        in_specs=[sm,sm,vm,vm,vm],out_specs=(vm,vm),
        scratch_shapes=[pltpu.VMEM((8,BLK),f32),pltpu.VMEM((HN,80,BLK),f32)],
        compiler_params=pltpu.CompilerParams(vmem_limit_bytes=48<<20),
        name="tree_attention",
    )(path,cnt,qt,k,vt)

def bwd_kernel(path_ref,cnt_ref,qt_ref,k_ref,v_ref,kt_ref,dot_ref,o_ref,lse_ref,dqt_ref,dk_ref,dv_ref,dq_s):
    nt=(((1,),(1,)),((),()))
    dk_ref[...]=jnp.zeros_like(dk_ref); dv_ref[...]=jnp.zeros_like(dv_ref)
    def qblock(i,_):
        qs=pl.ds(pl.multiple_of(i*BLK,BLK),BLK)
        qm=[_masked(qt_ref[h*HD:(h+1)*HD,qs],h) for h in range(HN)]
        dt=[dot_ref[h*HD:(h+1)*HD,qs] for h in range(HN)]
        dm=[_masked(dt[h],h) for h in range(HN)]
        delta=[jnp.sum(dt[h].astype(f32)*o_ref[h*HD:(h+1)*HD,qs],axis=0,keepdims=True) for h in range(HN)]
        lse=[lse_ref[h:h+1,qs] for h in range(HN)]
        def keys(ks,first):
            ps=[];ds=[]
            for h in range(HN):
                s=jnp.dot(k_ref[ks,_lanes(h)],qm[h],preferred_element_type=f32)*LOG2E
                p=jnp.exp2(s-lse[h])
                dp=jnp.dot(v_ref[ks,_lanes(h)],dm[h],preferred_element_type=f32)
                d=(p*(dp-delta[h])).astype(bf)
                ps.append(p.astype(bf)); ds.append(d)
                g=jnp.dot(kt_ref[h*HD:(h+1)*HD,ks],d,preferred_element_type=f32)
                if first: dq_s[h]=g
                else: dq_s[h]+=g
            dv_ref[ks,0:128]+=lax.dot_general(jnp.concatenate(ps[:2],1),jnp.concatenate(dm[:2],1),nt,preferred_element_type=f32)
            dk_ref[ks,0:128]+=lax.dot_general(jnp.concatenate(ds[:2],1),jnp.concatenate(qm[:2],1),nt,preferred_element_type=f32)
            dv_ref[ks,128:192]+=lax.dot_general(ps[2],dm[2],nt,preferred_element_type=f32)
            dk_ref[ks,128:192]+=lax.dot_general(ds[2],qm[2],nt,preferred_element_type=f32)
        for t in range(TRUNK//TCH):
            keys(slice(t*TCH,(t+1)*TCH),t==0)
        def step(j,_):
            kb=path_ref[i,j]
            keys(pl.ds(pl.multiple_of(kb*BLK,BLK),BLK),False)
            return 0
        lax.fori_loop(0,cnt_ref[i],step,0)
        for h in range(HN):
            dqt_ref[h*HD:(h+1)*HD,qs]=(dq_s[h]*0.125).astype(bf)
        return 0
    lax.fori_loop(0,NB,qblock,0)
TCH=512
def attn_bwd(path,cnt,qt,k,v,kt,dot,o,lse):
    S=qt.shape[1]
    vm=pl.BlockSpec(memory_space=pltpu.VMEM); sm=pl.BlockSpec(memory_space=pltpu.SMEM)
    return pl.pallas_call(bwd_kernel,
        out_shape=(jax.ShapeDtypeStruct((HN*HD,S),bf),jax.ShapeDtypeStruct((S,HN*HD),f32),jax.ShapeDtypeStruct((S,HN*HD),f32)),
        in_specs=[sm,sm]+[vm]*7,out_specs=(vm,vm,vm),
        scratch_shapes=[pltpu.VMEM((HN,HD,BLK),f32)],
        compiler_params=pltpu.CompilerParams(vmem_limit_bytes=56<<20),
        name="tree_attention_grad",
    )(path,cnt,qt,k,v,kt,dot,o,lse)

def path_tables(parent):
    segs=parent.shape[0]
    seg=jnp.maximum(jnp.arange(NB)-3,0).astype(jnp.int32)
    cols=[];cnt=jnp.zeros((NB,),jnp.int32);cur=seg
    for _ in range(segs-1):
        cols.append(jnp.maximum(cur+3,0)); cnt=cnt+(cur>0)
        nxt=jnp.sum(jnp.where(cur[:,None]==jnp.arange(segs)[None,:],parent[None,:],0),axis=1).astype(jnp.int32)
        cur=jnp.where(cur>0,nxt,0)
    return jnp.stack(cols,1),cnt


D = 768
SEQ = 4096
ROWS = SEQ // 4
QW = HN * HD
FQ = 768
epsilon = 1e-05
root_half = 0.7071067811865476
inv_root_tau = 0.3989422804014327


def layer_norm(summed, gain_row, shift_row):
    centre = jnp.mean(summed, axis=-1, keepdims=True)
    offset = summed - centre
    inv_std = lax.rsqrt(jnp.mean(offset * offset, axis=-1, keepdims=True) + epsilon)
    normed = offset * inv_std
    return normed * gain_row + shift_row, normed, inv_std


def norm_back(grad_out, normed, inv_std, gain_row):
    scaled = grad_out * gain_row
    return inv_std * (
        scaled
        - jnp.mean(scaled, axis=-1, keepdims=True)
        - normed * jnp.mean(scaled * normed, axis=-1, keepdims=True)
    )


def gelu_parts(u):
    half = 0.5 * (1.0 + lax.erf(u * root_half))
    return u * half, half + u * inv_root_tau * jnp.exp(-0.5 * u * u)


def partner(x, mask):
    return lax.ppermute(x, "tensor", [(i, i ^ mask) for i in range(4)])


def on_device(
    input_rows, time_embed, parents, qkv_weight, qv_bias, out_weight, out_bias, inner_weight,
    inner_bias, outer_weight, outer_bias, norm_gain, norm_shift, cotangent,
):
    rank = lax.axis_index("tensor")
    part = qkv_weight.shape[0]
    wide = dict(preferred_element_type=f32)

    start_sum = input_rows.astype(f32) + time_embed.astype(f32)
    start_low = start_sum.astype(bf)
    across = partner(start_low, 2)
    both = partner(jnp.stack([start_low, across]), 1)
    whole = jnp.zeros((SEQ, D), bf)
    for m, piece in ((0, start_low), (2, across), (1, both[0]), (3, both[1])):
        whole = lax.dynamic_update_slice_in_dim(whole, piece, (rank ^ m) * ROWS, 0)

    qkv_all = lax.all_gather(qkv_weight.reshape(part, 3 * QW), "dp", axis=0, tiled=True)
    packed = jnp.concatenate([inner_weight, outer_weight.T, out_weight.T], axis=1)
    packed = lax.all_gather(packed, "dp", axis=0, tiled=True)
    packed = lax.all_gather(packed, "tensor", axis=0, tiled=False)

    bias = qv_bias.astype(f32)
    wq, wk, wv = (qkv_all[:, i * QW:(i + 1) * QW] for i in range(3))
    tr = lambda w: lax.dot_general(w, whole, (((0,), (1,)), ((), ())), **wide)
    qt = ((tr(wq) + bias[0][:, None]).astype(bf).astype(f32) * 0.125).astype(bf)
    k = jnp.dot(whole, wk, **wide).astype(bf)
    v = (jnp.dot(whole, wv, **wide) + bias[1]).astype(bf)
    kt, vt = k.T, v.T
    vt_ext = jnp.concatenate(
        [vt.reshape(HN, HD, SEQ), jnp.ones((HN, 1, SEQ), bf), jnp.zeros((HN, 15, SEQ), bf)], 1)
    path, cnt = path_tables(parents[0])
    ot, lse = attn_fwd(path, cnt, qt, k, vt_ext)
    mix_low = ot.astype(bf)

    def to_tokens(x):
        out = jnp.zeros((D, ROWS), bf)
        for m in range(4):
            piece = lax.dynamic_slice_in_dim(x, (rank ^ m) * ROWS, ROWS, 1)
            piece = partner(piece, m) if m else piece
            out = lax.dynamic_update_slice_in_dim(out, piece, (rank ^ m) * QW, 0)
        return out

    def to_heads(x):
        out = jnp.zeros((QW, SEQ), bf)
        for m in range(4):
            piece = lax.dynamic_slice_in_dim(x, (rank ^ m) * QW, QW, 0)
            piece = partner(piece, m) if m else piece
            out = lax.dynamic_update_slice_in_dim(out, piece, (rank ^ m) * ROWS, 1)
        return out

    mixed = to_tokens(mix_low)
    inner = [packed[t, :, :FQ] for t in range(4)]
    outer_t = [packed[t, :, FQ:2 * FQ] for t in range(4)]
    out_t = jnp.concatenate([packed[t, :, 2 * FQ:] for t in range(4)], axis=1)
    bias_in = lax.all_gather(inner_bias, "tensor", axis=0, tiled=False).astype(f32)
    gain, shift = norm_gain.astype(f32), norm_shift.astype(f32)

    attn_out = lax.dot_general(mixed, out_t, (((0,), (1,)), ((), ())), **wide) + out_bias.astype(f32)
    hidden, normed1, inv1 = layer_norm(start_sum + attn_out, gain[0], shift[0])
    hidden_low = hidden.astype(bf)
    acts, slopes = [], []
    mlp = outer_bias.astype(f32)
    for t in range(4):
        u = jnp.dot(hidden_low, inner[t], **wide) + bias_in[t]
        value, slope = gelu_parts(u)
        acts.append(value.astype(bf))
        slopes.append(slope)
        mlp = mlp + jnp.einsum("tf,df->td", acts[t], outer_t[t], **wide)
    final, normed2, inv2 = layer_norm(hidden + mlp, gain[1], shift[1])
    block_out = final.astype(bf)

    grad_final = cotangent.astype(f32)
    gain2 = jnp.sum(grad_final * normed2, axis=0)
    shift2 = jnp.sum(grad_final, axis=0)
    grad2 = norm_back(grad_final, normed2, inv2, gain[1])
    gm = grad2.astype(bf)
    outer_bias_sum = jnp.sum(gm, axis=0, dtype=f32)
    gin = grad2
    inner_sums, grads = [], []
    for t in range(4):
        gp = (jnp.dot(gm, outer_t[t], **wide) * slopes[t]).astype(bf)
        inner_sums.append(jnp.sum(gp, axis=0, dtype=f32))
        gin = gin + jnp.einsum("tf,df->td", gp, inner[t], **wide)
        dinner = jnp.einsum("td,tf->df", hidden_low, gp, **wide)
        douter = jnp.einsum("td,tf->df", gm, acts[t], **wide)
        grads.append([dinner.astype(bf), douter.astype(bf)])
    gain1 = jnp.sum(gin * normed1, axis=0)
    shift1 = jnp.sum(gin, axis=0)
    grad1 = norm_back(gin, normed1, inv1, gain[0])
    ga = grad1.astype(bf)
    out_bias_sum = jnp.sum(ga, axis=0, dtype=f32)
    dout = jnp.einsum("td,ct->dc", ga, mixed, **wide).astype(bf)
    for t in range(4):
        grads[t] = jnp.concatenate(grads[t] + [dout[:, t * QW:(t + 1) * QW]], axis=1)
    share = lax.psum_scatter(jnp.stack(grads), "tensor", scatter_dimension=0, tiled=False)
    share = lax.psum_scatter(share, "dp", scatter_dimension=0, tiled=True).astype(f32)

    do_t = to_heads(jnp.einsum("dc,td->ct", out_t, ga, **wide).astype(bf))
    dqt, dk, dv = attn_bwd(path, cnt, qt, k, v, kt, do_t, ot, lse)
    dq = dqt.T
    dk, dv = dk.astype(bf), dv.astype(bf)
    grad_proj = jnp.concatenate([dq, dk, dv], axis=1)
    dqkv = jnp.einsum("td,tf->df", whole, grad_proj, **wide).astype(bf)
    qkv_share = lax.psum_scatter(dqkv, "dp", scatter_dimension=0, tiled=True).astype(f32)
    partial = jnp.einsum("tf,df->td", grad_proj, qkv_all, **wide).astype(bf).reshape(4, ROWS, D)
    take = lambda i: lax.dynamic_index_in_dim(partial, i, 0, keepdims=False)
    got = partner(jnp.stack([take(rank ^ 1), take(rank ^ 3)]), 1).astype(f32)
    far = partner((take(rank ^ 2).astype(f32) + got[1]).astype(bf), 2).astype(f32)
    input_grad = (take(rank).astype(f32) + got[0] + far + grad1).astype(bf)

    pair = jnp.stack([jnp.sum(dq, axis=0, dtype=f32), jnp.sum(dv, axis=0, dtype=f32)])
    pair = lax.dynamic_update_slice_in_dim(jnp.zeros((2, D), f32), pair, rank * QW, 1)
    sums = lax.psum(
        jnp.concatenate(
            [pair, jnp.stack(inner_sums), jnp.stack([out_bias_sum, outer_bias_sum, gain1, gain2, shift1, shift2])]),
        ("dp", "tensor"))
    return (
        block_out,
        input_grad,
        qkv_share.reshape(part, 3, QW),
        lax.dynamic_slice_in_dim(sums[:2], rank * QW, QW, 1),
        share[:, 2 * FQ:].T,
        sums[6],
        share[:, :FQ],
        lax.dynamic_index_in_dim(sums[2:6], rank, 0, keepdims=False),
        share[:, FQ:2 * FQ].T,
        sums[7],
        sums[8:10],
        sums[10:12],
    )


def solution(mesh):
    both = P(("dp", "tensor"), None)
    return jax.shard_map(
        on_device,
        mesh=mesh,
        in_specs=(
            both, P("dp", None), P("dp", None), P("dp", None, "tensor"), P(None, "tensor"),
            P("tensor", "dp"), P(), P("dp", "tensor"), P("tensor"), P("tensor", "dp"), P(), P(), P(), both,
        ),
        out_specs=(
            both, both, P("dp", None, "tensor"), P(None, "tensor"), P("tensor", "dp"), P(),
            P("dp", "tensor"), P("tensor"), P("tensor", "dp"), P(), P(), P(),
        ),
        check_vma=False,
    )
```

time: 1960 us -> 680 us (0.35)
  matrix products: 801 us -> 109 us
  waiting for transfers between devices: 536 us -> 154 us
  other arithmetic: 316 us -> 42.8 us
  Pallas kernels: 0 us -> 136 us
  local copies, waits for them, and re-layouts: 142 us -> 75.2 us
  blocking collectives: 114 us -> 141 us
  loops' own time: 22.8 us -> 0 us
    dot_general x66 -> x32, matrix products: 788 us -> 109 us  [the longest x4 15.3 us: on_device(): mlp = mlp + jnp.einsum('tf,df->td', acts[t], outer_t[t], **wide)]
    reduce_scatter x7 -> x2, waiting for transfers between devices: 366 us -> 0.01 us  [the longest x1 0.01 us: on_device(): lax.psum_scatter(jnp.stack(grads), 'tensor', scatter_dimension=0, tiled=F...]
    convert_element_type x19 -> x12, other arithmetic: 190 us -> 17.1 us  [the longest x1 5.07 us: on_device(): input_grad = (take(rank).astype(f32) + got[0] + far + grad1).astype(bf)]
    pallas_call x0 -> x2, Pallas kernels: none -> 136 us  [the longest x1 80 us: attn_bwd(): pl.pallas_call(bwd_kernel, out_shape=(jax.ShapeDtypeStruct((HN * HD, S),...]
    all_gather x6 -> x2, waiting for transfers between devices: 169 us -> 59.5 us  [the longest x1 59.5 us: on_device(): packed = lax.all_gather(packed, 'dp', axis=0, tiled=True)]
    reduce_sum x16, other arithmetic: 118 us -> 10.6 us  [the longest x1 2.6 us: on_device(): outer_bias_sum = jnp.sum(gm, axis=0, dtype=f32)]
    ppermute x0 -> x10, waiting for transfers between devices: none -> 76.5 us  [partner(): return lax.ppermute(x, 'tensor', [(i, i ^ mask) for i in range(4)])]
    broadcast_in_dim x34 -> x5, local copies, waits for them, and re-layouts: 56.1 us -> 1.12 us  [the longest x1 0.77 us: on_device(): whole = jnp.zeros((SEQ, D), bf)]
  transfers between devices with their start and end apart: 14 -> 15, of which waited for: 10 -> 5; matrix products, arithmetic and copies ran while one was open for 42% -> 18% of each run, Pallas kernels for 0% -> 20%
where the time goes in v1:
time: 680 us; the launch traced here: 682 us
  waiting for transfers between devices  154 us (23%)
  blocking collectives  141 us (21%)
  Pallas kernels  136 us (20%)
  matrix products  109 us (16%)
  local copies, waits for them, and re-layouts  75.2 us (11%)
  other arithmetic  42.8 us (6%)
  between operations  15.3 us (2%)
  starting transfers between devices  8.87 us (1%)
    psum x1, blocking collectives, on_device(): lax.psum(jnp.concatenate([pair, jnp.stack(inner_sums), jnp.stack([out_bia...  89.9 us
    pallas_call x1, Pallas kernels, attn_bwd(): pl.pallas_call(bwd_kernel, out_shape=(jax.ShapeDtypeStruct((HN * HD, S),...  80 us
    ppermute x10, waiting for transfers between devices, partner(): return lax.ppermute(x, 'tensor', [(i, i ^ mask) for i in range(4)])  76.5 us
    all_gather x1, waiting for transfers between devices, on_device(): packed = lax.all_gather(packed, 'dp', axis=0, tiled=True)  59.5 us
    pallas_call x1, Pallas kernels, attn_fwd(): pl.pallas_call(fwd_kernel, out_shape=(jax.ShapeDtypeStruct((HN * HD, S),...  56.1 us
    unnamed x154, local copies, waits for them, and re-layouts  39 us
    all_gather x1, blocking collectives, on_device(): lax.all_gather(qkv_weight.reshape(part, 3 * QW), 'dp', axis=0, tiled=True)  33.4 us
    all_gather x1, blocking collectives, on_device(): lax.all_gather(inner_bias, 'tensor', axis=0, tiled=False).astype(f32)  17.9 us
  transfers between devices with their start and end apart: 15, of which 5 were waited for; matrix products, arithmetic and copies ran while one was open for 18% of the time, Pallas kernels for 20%

profile of v1, /device:TPU:0, one launch (start us, length us, event | category | flops | bytes accessed | tf_op | source)
XLA Modules:
  0.0 682.1 jit_solution(16158877946344898610)
XLA Ops:
  10.1 59.5 %all-gather.6.cloned.1.call-done = bf16[768,1728]{1,0:T(8,128)(2,1)} async-done(((bf16[96,1728]{1,0:T(8,128)(2,1)}), bf16[768,1728]{1,0:T(8,128)(2,1)}) %all-gather.6.cloned.1.call-update) | async-done | bytes 2654224 | tf_op jit(solution)/shard_map/all_gather | solution.py:176
  74.6 59.4 %collective-permute-done = bf16[1024,768]{0,1:T(8,128)(2,1)S(1)} collective-permute-done((bf16[1024,768]{0,1:T(8,128)(2,1)S(1)}, bf16[1024,768]{0,1:T(8,128)(2,1)S(1)}, u32[]{:S(2)}, u32[]{:S(2)}) %collective-permute-start) | collective-permute-done | bytes 1572896 | tf_op jit(solution)/shard_map/ppermute | solution.py:155
  138.6 33.4 %all_gather.18 = bf16[768,576]{1,0:T(8,128)(2,1)S(1)} all-gather(bf16[96,576]{1,0:T(8,128)(2,1)S(1)} %copy.148), channel_id=1, replica_groups=mesh['dp'=8,'tensor'=4] {'dp'}, dimensions={0}, use_global_device_ids=true | all-gather | bytes 995328 | tf_op jit(solution)/shard_map/all_gather | solution.py:174
  173.4 2.7 fusion.43
  176.1 2.7 fusion.42
  178.8 4.7 fusion.v_ref
  183.5 2.7 copy.150
  186.3 5.5 convolution_convert_fusion.1
  191.7 3.1 copy.151.k_ref
  194.9 5.1 fusion.5.qt_ref
  200.5 56.1 %tree_attention.1 = (f32[192,4096]{1,0:T(8,128)}, f32[8,4096]{1,0:T(8,128)S(1)}) custom-call(s32[16,12]{1,0:T(8,128)S(1)} %stack.83.path_ref, s32[16]{0:T(128)S(1)} %fusion.72.cnt_ref, bf16[192,4096]{1,0:T(8,128)(2,1)S(1)} %fusion.5.qt_ref, bf16[4096,192]{1,0:T(8,128)(2,1)S(1)} %copy.151.k_ref, bf16[3,80,4096]{2,1,0:T(8,128)(2,1)S(1)} %maximum_maximum_fusion.vt_ref), custom_call_target="tpu_custom_call" | custom-call | tf_op jit(solution)/shard_map/tree_attention/pallas_call | solution.py:55
  261.2 2.7 collective-permute-start.3
  265.4 17.9 %all-gather.2 = bf16[4,1,768]{2,1,0:T(2,128)(2,1)S(1)} all-gather(bf16[1,1,768]{2,1,0:T(2,128)(2,1)S(1)} %reshape.661), channel_id=3, replica_groups=mesh['dp'=8,'tensor'=4] {'tensor'}, dimensions={0}, use_global_device_ids=true | all-gather | bytes 7680 | tf_op jit(solution)/shard_map/all_gather | solution.py:212
  299.4 3.4 multiply_convert_fusion.1
  302.8 3.1 fusion.53
  305.9 3.4 multiply_convert_fusion.2
  309.3 3.0 fusion.50
  312.4 3.6 multiply_convert_fusion.3
  316.1 3.1 fusion.47
  319.2 6.1 fusion.86
  327.7 2.6 convert_reduce_fusion.3
  334.3 2.6 convolution_convert_fusion.10
  336.9 2.7 convolution_convert_fusion.3
  339.7 3.9 convert_reduce_fusion.5
  343.6 3.5 convert_reduce_fusion.8
  351.5 3.5 convert_reduce_fusion.7
  359.4 3.5 convert_reduce_fusion.6
  369.4 5.6 multiply_reduce_fusion
  381.7 5.1 pad_maximum_fusion
  386.9 2.8 convolution_convert_fusion.2
  392.3 10.2 %collective-permute-done.6 = bf16[192,1024]{1,0:T(8,128)(2,1)S(1)} collective-permute-done((bf16[192,1024]{1,0:T(8,128)(2,1)S(1)}, bf16[192,1024]{1,0:T(8,128)(2,1)S(1)}, u32[]{:S(2)}, u32[]{:S(2)}) %collective-permute-start.6) | collective-permute-done | bytes 393248 | tf_op jit(solution)/shard_map/ppermute | solution.py:155
  402.5 6.9 %collective-permute-done.7 = bf16[192,1024]{1,0:T(8,128)(2,1)S(1)} collective-permute-done((bf16[192,1024]{1,0:T(8,128)(2,1)S(1)}, bf16[192,1024]{1,0:T(8,128)(2,1)S(1)}, u32[]{:S(2)}, u32[]{:S(2)}) %collective-permute-start.7) | collective-permute-done | bytes 393248 | tf_op jit(solution)/shard_map/ppermute | solution.py:155
  410.6 80.0 %tree_attention_grad.1 = (bf16[192,4096]{1,0:T(8,128)(2,1)}, f32[4096,192]{1,0:T(8,128)}, f32[4096,192]{1,0:T(8,128)}) custom-call(s32[16,12]{1,0:T(8,128)} %copy-done.3, s32[16]{0:T(128)} %copy-done.4, bf16[192,4096]{1,0:T(8,128)(2,1)} %copy-done.1, bf16[4096,192]{1,0:T(8,128)(2,1)} %copy-done, bf16[4096,192]{1,0:T(8,128)(2,1)} %copy-done.7, ...), custom_call_target="tpu_custom_call" | custom-call | tf_op jit(solution)/shard_map/tree_attention_grad/pallas_call | solution.py:103
  490.6 3.9 copy.163
  500.1 8.9 %fusion.44 = bf16[768,576]{1,0:T(8,128)(2,1)} fusion(bf16[4096,768]{0,1:T(8,128)(2,1)} %fusion.42, bf16[4096,192]{1,0:T(8,128)(2,1)S(1)} %get-tuple-element.93, bf16[4096,192]{1,0:T(8,128)(2,1)S(1)} %convert_element_type.256, bf16[4096,192]{1,0:T(8,128)(2,1)S(1)} %bitcast.160), kind=kOutput, calls=%fused_computation.108 | convolution fusion | flops 3638476800 | bytes 11894784 | tf_op jit(solution)/shard_map/td,tf->df/dot_general | solution.py:260
  509.1 7.8 %convolution_convert_fusion = bf16[4096,768]{1,0:T(8,128)(2,1)S(1)} fusion(bf16[768,576]{1,0:T(8,128)(2,1)} %copy-done.28, bf16[4096,192]{1,0:T(8,128)(2,1)} %copy-done.16, bf16[4096,192]{1,0:T(8,128)(2,1)} %copy-done.15, bf16[4096,192]{1,0:T(8,128)(2,1)} %bitcast.159), kind=kOutput, calls=%fused_computation.1 | convolution fusion | flops 3641180160 | bytes 11894784 | tf_op jit(solution)/shard_map/tf,df->td/dot_general | solution.py:262
  516.9 2.8 constant_dynamic-slice_fusion.3
  519.7 2.6 copy.187
  522.3 2.6 copy.186
  524.9 3.9 pad_maximum_fusion.3
  529.2 4.6 copy.183
  533.8 2.6 copy.188
  536.4 2.7 convert_element_type.260
  544.2 2.6 copy.169
  549.2 89.9 %psum.7 = f32[12,768]{1,0:T(8,128)S(1)} all-reduce(f32[12,768]{1,0:T(8,128)S(1)} %concatenate.31), channel_id=1, replica_groups=mesh['dp'=8,'tensor'=4] {'dp','tensor'}, use_global_device_ids=true, to_apply=%region_32.33 | all-reduce | flops 9216 | bytes 73728 | tf_op jit(solution)/shard_map/psum | solution.py:270
  639.2 2.6 copy.185
  646.2 5.1 fusion.37
  653.8 17.7 %reduce-scatter.10.cloned.1.call-done = bf16[96,1728]{1,0:T(8,128)(2,1)} async-done(((bf16[768,1728]{1,0:T(8,128)(2,1)}), bf16[96,1728]{1,0:T(8,128)(2,1)}) %reduce-scatter.10.cloned.1.call-update) | async-done | bytes 331792
  (308 shorter events, 92.3 us)
Async XLA Ops:
  7.2 62.5 %copy-start.17 = (bf16[1024,768]{1,0:T(8,128)(2,1)S(1)}, bf16[1024,768]{1,0:T(8,128)(2,1)}, u32[]{:S(2)}) copy-start(bf16[1024,768]{1,0:T(8,128)(2,1)} %param.14) | copy-start | bytes 4718596
  7.2 62.4 %all-gather.6.cloned.1.call-start = ((), (), s32[]{:S(2)}) async-start(), calls=%async_computation.3 | async-start | bytes 3096576 | tf_op jit(solution)/shard_map/all_gather | solution.py:176
  10.0 60.4 %copy-start.49 = (bf16[1,768]{1,0:T(2,128)(2,1)S(1)}, bf16[1,768]{1,0:T(2,128)(2,1)}, u32[]{:S(2)}) copy-start(bf16[1,768]{1,0:T(2,128)(2,1)} %param.15) | copy-start | bytes 4612
  10.0 281.5 %all-gather.8.cloned.1.call-start = ((), (), s32[]{:S(2)}) async-start(), calls=%async_computation.6 | async-start | bytes 13762560 | tf_op jit(solution)/shard_map/all_gather | solution.py:177
  69.6 459.7 %reduce-scatter.8.cloned.1.call-start = ((), (), s32[]{:S(2)}) async-start(), calls=%async_computation.5 | async-start | bytes 13271040 | tf_op jit(solution)/shard_map/reduce_scatter | solution.py:252
  71.9 64.1 %copy-start.8 = (bf16[4096,768]{0,1:T(8,128)(2,1)}, bf16[4096,768]{0,1:T(8,128)(2,1)S(1)}, u32[]{:S(2)}) copy-start(bf16[4096,768]{0,1:T(8,128)(2,1)S(1)} %get-tuple-element.94) | copy-start | bytes 18874372
  71.9 62.1 %collective-permute-start = (bf16[1024,768]{0,1:T(8,128)(2,1)S(1)}, bf16[1024,768]{0,1:T(8,128)(2,1)S(1)}, u32[]{:S(2)}, u32[]{:S(2)}) collective-permute-start(bf16[1024,768]{0,1:T(8,128)(2,1)S(1)} %get-tuple-element.95), channel_id=1, source_target_pairs={{0,2},{1,3},{2,0},{3,1},{4,6},{5,7},{6,4},{7,5},{8,10},{9,11},{10,... | collective-permute-start | bytes 4718600 | tf_op jit(solution)/shard_map/ppermute | solution.py:155
  134.0 4.0 copy-start.32
  134.0 4.5 copy-start.48
  136.0 37.4 %collective-permute-start.1 = (bf16[2,1024,768]{1,2,0:T(8,128)(2,1)}, bf16[2,1024,768]{1,2,0:T(8,128)(2,1)}, u32[]{:S(2)}, u32[]{:S(2)}) collective-permute-start(bf16[2,1024,768]{1,2,0:T(8,128)(2,1)} %pad_maximum_fusion.2), channel_id=1, source_target_pairs={{0,1},{1,0},{2,3},{3,2},{4,5},{5,4},{6,7},{7,6},{8,9},{9,8},{10,11... | collective-permute-start | bytes 9437192 | tf_op jit(solution)/shard_map/ppermute | solution.py:155
  138.6 61.9 %copy-start.3 = (s32[16,12]{1,0:T(8,128)}, s32[16,12]{1,0:T(8,128)S(1)}, u32[]{:S(2)}) copy-start(s32[16,12]{1,0:T(8,128)S(1)} %stack.83.path_ref) | copy-start | bytes 2308
  138.6 61.9 %copy-start.4 = (s32[16]{0:T(128)}, s32[16]{0:T(128)S(1)}, u32[]{:S(2)}) copy-start(s32[16]{0:T(128)S(1)} %fusion.72.cnt_ref) | copy-start | bytes 196
  172.0 22.9 %copy-start.28 = (bf16[768,576]{1,0:T(8,128)(2,1)}, bf16[768,576]{1,0:T(8,128)(2,1)S(1)}, u32[]{:S(2)}) copy-start(bf16[768,576]{1,0:T(8,128)(2,1)S(1)} %all_gather.18) | copy-start | bytes 2654212
  194.9 5.6 copy-start
  194.9 5.1 copy-start.9
  200.0 56.6 %copy-start.1 = (bf16[192,4096]{1,0:T(8,128)(2,1)}, bf16[192,4096]{1,0:T(8,128)(2,1)S(1)}, u32[]{:S(2)}) copy-start(bf16[192,4096]{1,0:T(8,128)(2,1)S(1)} %fusion.5.qt_ref) | copy-start | bytes 4718596
  258.8 5.2 copy-start.51
  258.8 5.4 copy-start.54
  258.8 5.4 copy-start.52
  258.8 6.0 copy-start.53
  258.8 25.1 %copy-start.18 = (bf16[1024,768]{1,0:T(8,128)(2,1)S(1)}, bf16[1024,768]{1,0:T(8,128)(2,1)}, u32[]{:S(2)}) copy-start(bf16[1024,768]{1,0:T(8,128)(2,1)} %param.27) | copy-start | bytes 4718596
  261.2 24.9 %collective-permute-start.2 = (bf16[192,1024]{1,0:T(8,128)(2,1)}, bf16[192,1024]{1,0:T(8,128)(2,1)}, u32[]{:S(2)}, u32[]{:S(2)}) collective-permute-start(bf16[192,1024]{1,0:T(8,128)(2,1)} %get-tuple-element.115), channel_id=1, source_target_pairs={{0,1},{1,0},{2,3},{3,2},{4,5},{5,4},{6,7},{7,6},{8,9},{9,8},{10,11... | collective-permute-start | bytes 1179656 | tf_op jit(solution)/shard_map/ppermute | solution.py:155
  261.2 26.7 %collective-permute-start.3 = (bf16[192,1024]{1,0:T(8,128)(2,1)}, bf16[192,1024]{1,0:T(8,128)(2,1)}, u32[]{:S(2)}, u32[]{:S(2)}) collective-permute-start(bf16[192,1024]{1,0:T(8,128)(2,1)} %get-tuple-element.114), channel_id=1, source_target_pairs={{0,2},{1,3},{2,0},{3,1},{4,6},{5,7},{6,4},{7,5},{8,10},{9,11},{10,... | collective-permute-start | bytes 1179656 | tf_op jit(solution)/shard_map/ppermute | solution.py:155
  264.0 25.7 %collective-permute-start.4 = (bf16[192,1024]{1,0:T(8,128)(2,1)S(1)}, bf16[192,1024]{1,0:T(8,128)(2,1)}, u32[]{:S(2)}, u32[]{:S(2)}) collective-permute-start(bf16[192,1024]{1,0:T(8,128)(2,1)S(1)} %get-tuple-element.113), channel_id=1, source_target_pairs={{0,3},{1,2},{2,1},{3,0},{4,7},{5,6},{6,5},{7,4},{8,11},{9,10},{10,... | collective-permute-start | bytes 1179656 | tf_op jit(solution)/shard_map/ppermute | solution.py:155
  284.6 8.5 %copy-start.11 = (bf16[1024,768]{0,1:T(8,128)(2,1)S(1)}, bf16[1024,768]{0,1:T(8,128)(2,1)}, u32[]{:S(2)}) copy-start(bf16[1024,768]{0,1:T(8,128)(2,1)} %copy-done.10) | copy-start | bytes 4718596
  293.4 3.6 slice-start.1
  299.4 19.8 %copy-start.56 = (f32[1024,768]{1,0:T(8,128)}, f32[1024,768]{1,0:T(8,128)S(1)}, u32[]{:S(2)}) copy-start(f32[1024,768]{1,0:T(8,128)S(1)} %fusion.54) | copy-start | bytes 9437188
  302.8 3.1 copy-start.39
  316.0 3.1 copy-start.58
  332.8 6.9 %slice-start.3 = ((s8[11010048]{0:T(1024)(128)(4,1)}), s8[4194304]{0:T(1024)(128)(4,1)S(1)}, s32[]{:S(2)}) async-start(s8[11010048]{0:T(1024)(128)(4,1)} %bitcast.181), calls=%async_computation.11 | async-start | bytes 8388608
  334.3 5.3 slice-start.4
  339.7 3.9 copy-start.62
  386.9 257.4 %reduce-scatter.6.cloned.1.call-start = ((), (), s32[]{:S(2)}) async-start(), calls=%async_computation.4 | async-start | bytes 1105920 | tf_op jit(solution)/shard_map/reduce_scatter | solution.py:261
  390.1 2.1 collective-permute-start.5
  390.5 12.0 %collective-permute-start.6 = (bf16[192,1024]{1,0:T(8,128)(2,1)S(1)}, bf16[192,1024]{1,0:T(8,128)(2,1)S(1)}, u32[]{:S(2)}, u32[]{:S(2)}) collective-permute-start(bf16[192,1024]{1,0:T(8,128)(2,1)S(1)} %get-tuple-element.110), channel_id=1, source_target_pairs={{0,2},{1,3},{2,0},{3,1},{4,6},{5,7},{6,4},{7,5},{8,10},{9,11},{10,... | collective-permute-start | bytes 1179656 | tf_op jit(solution)/shard_map/ppermute | solution.py:155
  392.2 17.2 %collective-permute-start.7 = (bf16[192,1024]{1,0:T(8,128)(2,1)S(1)}, bf16[192,1024]{1,0:T(8,128)(2,1)S(1)}, u32[]{:S(2)}, u32[]{:S(2)}) collective-permute-start(bf16[192,1024]{1,0:T(8,128)(2,1)S(1)} %get-tuple-element.109), channel_id=1, source_target_pairs={{0,3},{1,2},{2,1},{3,0},{4,7},{5,6},{6,5},{7,4},{8,11},{9,10},{10,... | collective-permute-start | bytes 1179656 | tf_op jit(solution)/shard_map/ppermute | solution.py:155
  494.5 3.4 copy-start.14
  509.0 162.5 %reduce-scatter.10.cloned.1.call-start = ((), (), s32[]{:S(2)}) async-start(), calls=%async_computation.7 | async-start | bytes 3096576
  528.8 7.6 %collective-permute-start.8 = (bf16[2,1024,768]{1,2,0:T(8,128)(2,1)}, bf16[2,1024,768]{1,2,0:T(8,128)(2,1)}, u32[]{:S(2)}, u32[]{:S(2)}) collective-permute-start(bf16[2,1024,768]{1,2,0:T(8,128)(2,1)} %pad_maximum_fusion.3), channel_id=1, source_target_pairs={{0,1},{1,0},{2,3},{3,2},{4,5},{5,4},{6,7},{7,6},{8,9},{9,8},{10,11... | collective-permute-start | bytes 9437192 | tf_op jit(solution)/shard_map/ppermute | solution.py:155
  539.2 3.1 copy-start.5
  539.2 4.9 copy-start.37
  539.2 4.9 copy-start.36
  539.2 4.9 copy-start.43
  539.2 4.9 copy-start.44
  539.2 4.9 copy-start.45
  539.2 4.9 copy-start.42
  539.3 4.9 copy-start.33
  542.3 103.8 %collective-permute-start.9 = (bf16[1024,768]{0,1:T(8,128)(2,1)}, bf16[1024,768]{0,1:T(8,128)(2,1)}, u32[]{:S(2)}, u32[]{:S(2)}) collective-permute-start(bf16[1024,768]{0,1:T(8,128)(2,1)} %fusion.41), channel_id=1, source_target_pairs={{0,2},{1,3},{2,0},{3,1},{4,6},{5,7},{6,4},{7,5},{8,10},{9,11},{10,... | collective-permute-start | bytes 4718600 | tf_op jit(solution)/shard_map/ppermute | solution.py:155
  (36 other events, 71.7 us)
Sparse Core Ops, SparseCore 0:
  10.8 58.7 all-gather.5
  71.1 96.6 all-gather.7
  387.0 94.6 reduce-scatter.7
  509.1 87.8 reduce-scatter.5
  600.8 70.7 reduce-scatter.9

commit v2 on v1

v2 whole, which is shorter than its diff:
```python
import functools
import jax, jax.numpy as jnp
from jax import lax
from jax.experimental import pallas as pl
from jax.experimental.pallas import tpu as pltpu
from jax.sharding import PartitionSpec as P
bf = jnp.bfloat16
f32 = jnp.float32
BLK = 256
TRUNK = 1024
NB = 16
HD = 64
HN = 3
SEGS = 13
PAD = 4
LIST = 192
TQ = 512
TK = 1024
FP = 4
BP = 4
BTQ = 1024
BTK = 256
VM = pl.BlockSpec(memory_space=pltpu.VMEM)
SM = pl.BlockSpec(memory_space=pltpu.SMEM)
HB = pl.BlockSpec(memory_space=pltpu.HBM)
NT = (((1,), (1,)), ((), ()))


def mm(a, b, dims=(((1,), (0,)), ((), ()))):
    return lax.dot_general(a, b, dims, preferred_element_type=f32)


def aligned(i, n):
    return pl.ds(pl.multiple_of(i * n, n), n)


def list_pairs(parents, cur, pairs):
    for s in range(1, SEGS):
        cur[s] = jnp.int32(s)

    def level(_, n):
        for s in range(1, SEGS):
            c = cur[s]
            pairs[0, n] = jnp.int32(s + 3)
            pairs[1, n] = c + 3
            cur[s] = jnp.where(c > 0, parents[c], 0)
            n = n + jnp.where(c > 0, 1, 0)
        for i in range(PAD - 1):
            pairs[0, n + i] = jnp.int32(NB)
            pairs[1, n + i] = jnp.int32(NB)
        return (n + PAD - 1) // PAD * PAD

    pairs[2, 0] = lax.fori_loop(0, SEGS - 1, level, jnp.int32(0))


PR = 1024


def fwd_kernel(parents, tab, x_hbm, w_hbm, b_ref, qt_hbm, kv_hbm, kt_hbm, o_hbm, mix_hbm, lse_ref, pairs,
               cur, m_s, acc_s, xs, w_s, wt_s, wr_s, br_s, qt_ref, kv_ref, kt_ref, vt_ref, o_ref, mix_ref, sem):
    def fetch(i, slot):
        return pltpu.make_async_copy(x_hbm.at[i], xs.at[slot], sem.at[slot])

    load_w = pltpu.make_async_copy(w_hbm, w_s, sem.at[2])
    load_w.start()
    fetch(0, 0).start()
    list_pairs(parents, cur, pairs)
    load_w.wait()
    bias = b_ref[...]
    w = w_s[...].reshape(w_s.shape[0] * w_s.shape[1], w_s.shape[2])
    wt_s[...] = w.T
    for h in range(HN):
        for c in (1, 2):
            to = slice(h * 128 + (c - 1) * HD, h * 128 + c * HD)
            wr_s[:, to] = w[:, c * HN * HD + h * HD:c * HN * HD + (h + 1) * HD]
            part = bias[:, HN * HD + h * HD:HN * HD + (h + 1) * HD] if c == 2 else jnp.zeros((1, HD), f32)
            br_s[:, to] = jnp.broadcast_to(part, (8, HD))
    bias_col = jnp.transpose(jnp.broadcast_to(bias, (8, 2 * HN * HD)))
    ones = (lax.broadcasted_iota(jnp.int32, (16, PR), 0) == 0).astype(f32).astype(bf)

    def rows(i, _):
        slot = lax.rem(i, 2)

        @pl.when(i + 1 < NB * BLK // PR)
        def _():
            fetch(i + 1, 1 - slot).start()

        fetch(i, slot).wait()
        cols = aligned(i, PR)
        x = xs[slot]
        up = mm(wt_s[...], x, NT)
        q = (up[:HN * HD] + bias_col[:HN * HD, 0:1]).astype(bf)
        qt_ref[:, cols] = (q.astype(f32) * 0.125).astype(bf)
        kt_ref[:, cols] = up[HN * HD:2 * HN * HD].astype(bf)
        vt = (up[2 * HN * HD:] + bias_col[HN * HD:, 0:1]).astype(bf)
        for h in range(HN):
            vt_ref[h, :HD, cols] = vt[h * HD:(h + 1) * HD]
            vt_ref[h, HD:, cols] = ones
        kv_ref[cols] = (mm(x, wr_s[...]) + br_s[0:1]).astype(bf)
        return 0

    lax.fori_loop(0, NB * BLK // PR, rows, 0)
    saves = [pltpu.make_async_copy(a, b, sem.at[3 + n])
             for n, (a, b) in enumerate(((qt_ref, qt_hbm), (kv_ref, kv_hbm), (kt_ref, kt_hbm)))]
    for c in saves:
        c.start()
    zero = jnp.zeros((HD, TQ), bf)

    def tile(i, _):
        qz = [jnp.concatenate([qt_ref[h * HD:(h + 1) * HD, aligned(i, TQ)], zero], 0) for h in range(HN)]
        m, acc = [None] * HN, [None] * HN
        for c in range(TRUNK // TK):
            ks = slice(c * TK, (c + 1) * TK)
            s = [mm(kv_ref[ks, h * 128:(h + 1) * 128], qz[h]) for h in range(HN)]
            new = [jnp.max(x, axis=0, keepdims=True) for x in s]
            if c:
                new = [jnp.maximum(x, y) for x, y in zip(m, new)]
            p = [jnp.exp(x - y).astype(bf) for x, y in zip(s, new)]
            a = [mm(vt_ref[h, :, ks], p[h]) for h in range(HN)]
            if c:
                a = [x * jnp.exp(y - z) + w for x, y, z, w in zip(acc, m, new, a)]
            m, acc = new, a
        for h in range(HN):
            for j in range(TQ // BLK):
                acc_s[i * (TQ // BLK) + j, h] = acc[h][:, j * BLK:(j + 1) * BLK]
                m_s[i * (TQ // BLK) + j, h:h + 1] = m[h][:, j * BLK:(j + 1) * BLK]
        return 0

    lax.fori_loop(0, NB * BLK // TQ, tile, 0)

    def step(g, _):
        work = []
        for p in range(FP):
            q, kb = pairs[0, g * FP + p], jnp.minimum(pairs[1, g * FP + p], NB - 1)
            work += [(q, aligned(jnp.minimum(q, NB - 1), BLK), aligned(kb, BLK), h) for h in range(HN)]
        s = [mm(kv_ref[ks, h * 128:(h + 1) * 128],
                jnp.concatenate([qt_ref[h * HD:(h + 1) * HD, qs], zero[:, :BLK]], 0)) for q, qs, ks, h in work]
        m = [m_s[q, h:h + 1] for q, qs, ks, h in work]
        new = [jnp.maximum(y, jnp.max(x, axis=0, keepdims=True)) for x, y in zip(s, m)]
        p = [jnp.exp(x - y).astype(bf) for x, y in zip(s, new)]
        a = [mm(vt_ref[h, :, ks], x) for x, (q, qs, ks, h) in zip(p, work)]
        a = [acc_s[q, h] * jnp.exp(x - y) + z for x, y, z, (q, qs, ks, h) in zip(m, new, a, work)]
        for x, y, (q, qs, ks, h) in zip(new, a, work):
            m_s[q, h:h + 1] = x
            acc_s[q, h] = y
        return 0

    lax.fori_loop(0, pairs[2, 0] // FP, step, 0)

    def finish(i, _):
        qs = aligned(i, BLK)
        for h in range(HN):
            total = acc_s[i, h, HD:HD + 1, :]
            out = acc_s[i, h, 0:HD, :] / total
            o_ref[h * HD:(h + 1) * HD, qs] = out
            mix_ref[tab[i // 4], h * HD:(h + 1) * HD, aligned(lax.rem(i, 4), BLK)] = out.astype(bf)
            lse_ref[h:h + 1, qs] = m_s[i, h:h + 1] + jnp.log(total)
        return 0

    lax.fori_loop(0, NB, finish, 0)
    saves += [pltpu.make_async_copy(mix_ref, mix_hbm, sem.at[6]), pltpu.make_async_copy(o_ref, o_hbm, sem.at[7])]
    for c in saves[3:]:
        c.start()
    for c in saves:
        c.wait()


def attn_fwd(parents, tab, whole, w, bias):
    S = NB * BLK
    sd = jax.ShapeDtypeStruct
    vm = pltpu.VMEM
    n = HN * HD
    d = whole.shape[2]
    return pl.pallas_call(
        fwd_kernel,
        out_shape=(sd((n, S), bf), sd((S, 2 * n), bf), sd((n, S), bf), sd((n, S), f32), sd((4, n, S // 4), bf),
                   sd((8, S), f32), sd((3, LIST), jnp.int32)),
        in_specs=[SM, SM, HB, HB, VM], out_specs=(HB,) * 5 + (VM, SM),
        scratch_shapes=[pltpu.SMEM((16,), jnp.int32), vm((NB + 1, 8, BLK), f32), vm((NB + 1, HN, 80, BLK), f32),
                        vm((2, PR, d), bf), vm(w.shape, bf), vm((3 * n, d), bf), vm((d, 2 * n), bf), vm((8, 2 * n), f32),
                        vm((n, S), bf), vm((S, 2 * n), bf), vm((n, S), bf), vm((HN, 80, S), bf),
                        vm((n, S), f32), vm((4, n, S // 4), bf), pltpu.SemaphoreType.DMA((8,))],
        compiler_params=pltpu.CompilerParams(vmem_limit_bytes=60 << 20),
        cost_estimate=pl.CostEstimate(flops=40_000_000_000, bytes_accessed=12_000_000, transcendentals=18_000_000),
        name="tree_attention",
    )(parents, tab, whole, w, bias)


def bwd_kernel(heads, pairs, tab, qt_hbm, kv_hbm, kt_hbm, dots_hbm, o_hbm, lse_ref, dqt_hbm, dkv_hbm,
               dkv_s, dq_s, st_s, dot_ref, qt_ref, kv_ref, kt_ref, dots, o_ref, dqt_ref, dkv_ref, sem):
    loads = [pltpu.make_async_copy(a, b, sem.at[n]) for n, (a, b) in enumerate((
        (dots_hbm, dots), (o_hbm, o_ref), (qt_hbm, qt_ref), (kv_hbm, kv_ref), (kt_hbm, kt_ref)))]
    for c in loads:
        c.start()
    dkv_s[...] = jnp.zeros_like(dkv_s)
    dq_s[...] = jnp.zeros_like(dq_s)
    loads[0].wait()
    for m in range(4):
        dot_ref[:, aligned(tab[m], NB * BLK // 4)] = dots[m]
    loads[1].wait()

    def stats(i, _):
        qs = aligned(i, BLK)
        for n, h in enumerate(heads):
            rows = slice(h * HD, (h + 1) * HD)
            st_s[i, n:n + 1] = jnp.sum(dot_ref[rows, qs].astype(f32) * o_ref[rows, qs], axis=0, keepdims=True)
            st_s[i, 4 + n:5 + n] = lse_ref[h:h + 1, qs]
        return 0

    lax.fori_loop(0, NB, stats, 0)
    for c in loads[2:]:
        c.wait()

    def chains(work, width):
        zero = jnp.zeros((HD, width), bf)
        rows = lambda h: slice(h * HD, (h + 1) * HD)
        qz = [jnp.concatenate([qt_ref[rows(h), qs], zero], 0) for h, qs, ks, lse, delta in work]
        dz = [jnp.concatenate([zero, dot_ref[rows(h), qs]], 0) for h, qs, ks, lse, delta in work]
        kv = [kv_ref[ks, h * 128:(h + 1) * 128] for h, qs, ks, lse, delta in work]
        p = [jnp.exp(mm(x, y) - w[3]) for x, y, w in zip(kv, qz, work)]
        ds = [(x * (mm(y, z) - w[4])).astype(bf) for x, y, z, w in zip(p, kv, dz, work)]
        g = [mm(jnp.concatenate([x, y.astype(bf)], 1), jnp.concatenate([z, u], 1), NT)
             for x, y, z, u in zip(ds, p, qz, dz)]
        return g, [mm(kt_ref[rows(h), ks], x) for x, (h, qs, ks, lse, delta) in zip(ds, work)]

    per = BTQ // BLK

    def tile(i, _):
        row = lambda k: jnp.concatenate([st_s[i * per + j, k:k + 1] for j in range(per)], 1)
        dq = [None] * len(heads)
        for c in range(TRUNK // BTK):
            ks = slice(c * BTK, (c + 1) * BTK)
            g, d = chains([(h, aligned(i, BTQ), ks, row(4 + n), row(n)) for n, h in enumerate(heads)], BTQ)
            for n in range(len(heads)):
                dkv_s[ks, n * 128:(n + 1) * 128] += g[n]
                dq[n] = d[n] if c == 0 else dq[n] + d[n]
        for n in range(len(heads)):
            for j in range(per):
                dq_s[i * per + j, n] += dq[n][:, j * BLK:(j + 1) * BLK]
        return 0

    lax.fori_loop(0, NB * BLK // BTQ, tile, 0)

    def step(s, _):
        work, where = [], []
        for p in range(BP):
            q, kb = pairs[0, s * BP + p], pairs[1, s * BP + p]
            qr = jnp.minimum(q, NB - 1)
            for n, h in enumerate(heads):
                work.append((h, aligned(qr, BLK), aligned(jnp.minimum(kb, NB - 1), BLK),
                             st_s[qr, 4 + n:5 + n], st_s[qr, n:n + 1]))
                where.append((q, kb, n))
        for g, d, (q, kb, n) in zip(*chains(work, BLK), where):
            dkv_s[aligned(kb, BLK), n * 128:(n + 1) * 128] += g
            dq_s[q, n] += d
        return 0

    lax.fori_loop(0, pairs[2, 0] // BP, step, 0)

    def finish(i, _):
        for n in range(len(heads)):
            dqt_ref[n * HD:(n + 1) * HD, aligned(i, BLK)] = (dq_s[i, n] * 0.125).astype(bf)
        dkv_ref[aligned(i, BLK)] = dkv_s[aligned(i, BLK)].astype(bf)
        return 0

    lax.fori_loop(0, NB, finish, 0)
    saves = [pltpu.make_async_copy(dqt_ref, dqt_hbm, sem.at[5]), pltpu.make_async_copy(dkv_ref, dkv_hbm, sem.at[6])]
    for c in saves:
        c.start()
    for c in saves:
        c.wait()


def attn_bwd(heads, pairs, tab, qt, kv, kt, dots, o, lse):
    S = qt.shape[1]
    sd = jax.ShapeDtypeStruct
    n = len(heads)
    return pl.pallas_call(
        functools.partial(bwd_kernel, heads),
        out_shape=(sd((n * HD, S), bf), sd((S, n * 128), bf)),
        in_specs=[SM, SM] + [HB] * 5 + [VM], out_specs=(HB, HB),
        scratch_shapes=[pltpu.VMEM((S + BLK, n * 128), f32), pltpu.VMEM((NB + 1, n, HD, BLK), f32),
                        pltpu.VMEM((NB, 8, BLK), f32), pltpu.VMEM((HN * HD, S), bf)]
        + [pltpu.VMEM(a.shape, a.dtype) for a in (qt, kv, kt, dots, o)]
        + [pltpu.VMEM((n * HD, S), bf), pltpu.VMEM((S, n * 128), bf), pltpu.SemaphoreType.DMA((7,))],
        compiler_params=pltpu.CompilerParams(vmem_limit_bytes=60 << 20),
        cost_estimate=pl.CostEstimate(flops=20_000_000_000 * n, bytes_accessed=8_000_000 * n, transcendentals=6_000_000 * n),
        name="tree_attention_grad",
    )(pairs, tab, qt, kv, kt, dots, o, lse)


D = 768
SEQ = 4096
ROWS = SEQ // 4
QW = HN * HD
FQ = 768
PK = 1792
MESH = pl.DeviceIdType.MESH
HBM = pl.BlockSpec(memory_space=pl.ANY)
TN = (((0,), (0,)), ((), ()))
epsilon = 1e-05
root_half = 0.7071067811865476
inv_root_tau = 0.3989422804014327


def layer_norm(summed, gain_row, shift_row):
    centre = jnp.mean(summed, axis=-1, keepdims=True)
    offset = summed - centre
    inv_std = lax.rsqrt(jnp.mean(offset * offset, axis=-1, keepdims=True) + epsilon)
    normed = offset * inv_std
    return normed * gain_row + shift_row, normed, inv_std


def norm_back(grad_out, normed, inv_std, gain_row):
    scaled = grad_out * gain_row
    return inv_std * (
        scaled
        - jnp.mean(scaled, axis=-1, keepdims=True)
        - normed * jnp.mean(scaled * normed, axis=-1, keepdims=True)
    )


def gelu_parts(u):
    half = 0.5 * (1.0 + lax.erf(u * root_half))
    return u * half, half + u * inv_root_tau * jnp.exp(-0.5 * u * u)


def partner(x, mask):
    return lax.ppermute(x, "tensor", [(i, i ^ mask) for i in range(4)])


def across_x(x):
    return lax.ppermute(x, "dp", [(i, i ^ 1) for i in range(8)])


def flip1(r):
    return r + 1 - 2 * lax.rem(r, 2)


CH = 4
CROWS = ROWS // CH


def remote(src, dst, s, q, dev):
    return pltpu.make_async_remote_copy(
        src_ref=src, dst_ref=dst, send_sem=s, recv_sem=q, device_id=dev, device_id_type=MESH)


def meet(targets, meanwhile=None):
    barrier = pltpu.get_barrier_semaphore()
    for t in targets:
        pl.semaphore_signal(barrier, inc=1, device_id=t, device_id_type=MESH)
    if meanwhile is not None:
        meanwhile()
    pl.semaphore_wait(barrier, len(targets))


class Sends:
    def __init__(self):
        self.started = []

    def go(self, *args):
        c = remote(*args)
        c.start()
        self.started.append(c)
        return c

    def drain(self):
        for c in self.started:
            c.wait_send()


def gather_kernel(with_w, *refs):
    if with_w:
        (inp, te, wq, w1, w2, w3, bias, whole_hbm, wqg_hbm, gz_hbm, gx_hbm, whole, wqg, gz, gx, bcol,
         ysend, yrecv, csend, crecv, out, zsend, zrecv, xsend, xrecv) = refs
    else:
        inp, te, whole_hbm, whole, ysend, yrecv, csend, crecv, out = refs
    r = lax.axis_index("tensor")
    d = lax.axis_index("dp")
    rc, ry = flip1(r), lax.rem(r + 2, 4)
    core, yy = {"tensor": rc}, {"tensor": ry}
    targets = [core, yy]
    if with_w:
        z, x = d // 2, lax.rem(d, 2)
        xx = {"dp": flip1(d)}
        up, down = {"dp": lax.rem(z + 1, 4) * 2 + x}, {"dp": lax.rem(z + 3, 4) * 2 + x}
        targets += [xx, up, down]

    def prepare():
        shift = te[...].astype(f32)
        whole[r] = (inp[...].astype(f32) + shift).astype(bf)
        if with_w:
            for c in range(3):
                wqg[d, :, c * QW:(c + 1) * QW] = wq[c]

    meet(targets, prepare)
    sends = Sends()
    if with_w:

        def line(a, s, slot, way):
            ref = wqg.at[slot * 2 + x] if a == 0 else gz.at[slot]
            k = 2 * (s - 1) + way
            return remote(ref, ref, zsend.at[a, k], zrecv.at[a, k], (up, down)[way])

        def side(a, i, slot):
            src = wqg.at[slot * 2 + x] if a == 0 else gz.at[slot]
            dst = src if a == 0 else gx.at[slot]
            return remote(src, dst, xsend.at[a, i], xrecv.at[a, i], xx)

        def can_send(s, way):
            return jnp.logical_and(z < 3, z - s + 1 >= 0) if way == 0 else jnp.logical_and(z > 0, z + s - 1 <= 3)

        def can_recv(s, way):
            return z - s >= 0 if way == 0 else z + s <= 3

        def own(a):
            for way in (0, 1):
                @pl.when(can_send(1, way))
                def _():
                    line(a, 1, z, way).start()
            side(a, 0, z).start()

        own(0)
    rows = [pl.ds(i * CROWS, CROWS) for i in range(CH)]
    yc = []
    for i in range(CH):
        mine = whole.at[r, rows[i]]
        yc.append(sends.go(mine, mine, ysend.at[i], yrecv.at[i], yy))
    c0 = sends.go(whole.at[r], whole.at[r], csend.at[CH], crecv.at[CH], core)
    if with_w:
        part = wqg.shape[1]
        gz[z, :, 0:FQ] = w1[...]
        gz[z, :, FQ:2 * FQ] = w2[...]
        bcol[...] = jnp.transpose(jnp.broadcast_to(bias[...].astype(f32), (8, D)))
        fill = PK - 2 * FQ - QW
        column = bcol[pl.ds(pl.multiple_of(d * part, 32), part), 0:1]
        column = jnp.where(lax.broadcasted_iota(jnp.int32, (part, fill), 1) == 0, column, 0.0)
        gz[z, :, 2 * FQ:] = jnp.concatenate([w3[...].astype(f32).T, column], 1).astype(bf)
        own(1)
        for s in (1, 2, 3):
            for way in (0, 1):
                slot = z - s if way == 0 else z + s

                @pl.when(can_recv(s, way))
                def _():
                    for a in (0, 1):
                        line(a, s, slot, way).wait_recv()
                        if s < 3:
                            @pl.when(can_send(s + 1, way))
                            def _():
                                line(a, s + 1, slot, way).start()
                        side(a, slot_sem(s, way), slot).start()
    keeps = []

    def keep(src, dst):
        c = pltpu.make_async_copy(src, dst, out.at[len(keeps)])
        c.start()
        keeps.append(c)

    keep(whole.at[r], whole_hbm.at[r])
    cc = []
    for i in range(CH):
        yc[i].wait_recv()
        part = whole.at[ry, rows[i]]
        cc.append(sends.go(part, part, csend.at[i], crecv.at[i], core))
    keep(whole.at[ry], whole_hbm.at[ry])
    c0.wait_recv()
    keep(whole.at[rc], whole_hbm.at[rc])
    for c in cc:
        c.wait_recv()
    rd = 3 - r
    keep(whole.at[rd], whole_hbm.at[rd])
    if with_w:
        keep(gz, gz_hbm)
        for a in (0, 1):
            side(a, 0, z).wait()
        for s in (1, 2, 3):
            for way in (0, 1):
                slot = z - s if way == 0 else z + s

                @pl.when(can_recv(s, way))
                def _():
                    for a in (0, 1):
                        side(a, slot_sem(s, way), slot).wait()

                @pl.when(can_send(s, way))
                def _():
                    for a in (0, 1):
                        line(a, s, slot_of_send(z, s, way), way).wait_send()
        keep(gx, gx_hbm)
        keep(wqg, wqg_hbm)
    for c in keeps:
        c.wait()
    sends.drain()


def slot_of_send(z, s, way):
    return z - s + 1 if way == 0 else z + s - 1


def slot_sem(s, way):
    return 2 * s - 1 + way


def gather_start(inp, te, *weights):
    with_w = len(weights) > 0
    dma = pltpu.SemaphoreType.DMA
    shapes = [jax.ShapeDtypeStruct((4, ROWS, D), bf)]
    args = [inp, te, *weights]
    scratch = []
    sems = [dma((CH,)), dma((CH,)), dma((CH + 1,)), dma((CH + 1,)), dma((7,))]
    if with_w:
        part = weights[0].shape[1]
        line = jax.ShapeDtypeStruct((4, part, PK), bf)
        shapes += [jax.ShapeDtypeStruct((8, part, 3 * QW), bf), line, line]
        scratch = [pltpu.VMEM((D, 8), f32)]
        sems += [dma((2, 6)), dma((2, 6)), dma((2, 7)), dma((2, 7))]
    return pl.pallas_call(
        functools.partial(gather_kernel, with_w),
        out_shape=shapes, in_specs=[VM] * len(args), out_specs=[HB] * len(shapes),
        scratch_shapes=[pltpu.VMEM(a.shape, bf) for a in shapes] + scratch + sems,
        compiler_params=pltpu.CompilerParams(collective_id=0, has_side_effects=True, vmem_limit_bytes=60 << 20),
        name="gather_start",
    )(*args)


RB = 512
NR = ROWS // RB


def middle_kernel(with_w, *refs):
    if with_w:
        wa, wb, wc, wd = refs[:4]
        xsend, xrecv, wsend, wrecv = refs[-4:]
        refs = refs[4:-4]
    else:
        wfull, refs = refs[0], refs[1:]
    (mix_hbm, inp, te, cot, vec, block_out, grad1_o, dots_hbm, p00, p01, p10, p11, sums_o,
     w, wt_s, mix, mixr, gmix, dots, both, ht, gmt, gat, act, gp, slope_s,
     loc, asend, arecv, bsend, brecv, gsend, grecv) = refs
    r = lax.axis_index("tensor")
    d = lax.axis_index("dp")
    x = lax.rem(d, 2)
    ranks = [r, flip1(r), lax.rem(r + 2, 4), 3 - r]
    devices = [{"tensor": k} for k in ranks]
    xx = {"dp": flip1(d)}
    load = pltpu.make_async_copy(mix_hbm, mix, loc.at[5])
    load.start()
    meet(devices[1:] + ([xx] if with_w else []))
    sends = Sends()
    core = devices[1]
    load.wait()

    def heads_in(b, m):
        cols = pl.ds(b * RB, RB)
        return remote(mix.at[m, :, cols], mixr.at[m, :, cols], asend.at[b, m], arecv.at[b, m], devices[m])

    def heads_out(b, m):
        cols = aligned(b, RB)
        return remote(gmix.at[m, :, cols], dots.at[m, :, cols], bsend.at[b, m], brecv.at[b, m], devices[m])

    heads = [[heads_in(b, m) for m in (3, 2, 1)] for b in range(NR)]
    for c in heads[0]:
        c.start()
    fills, arrivals = [pltpu.make_async_copy(mix.at[0], mixr.at[0], loc.at[0])], []
    if with_w:
        ry = ranks[2]
        four, two, end = pl.ds(0, 4), pl.ds(0, 2), pl.ds(2, 2)
        own = ((wa, r, four, x), (wb, r, four, 1 - x), (wc, ry, four, x), (wd, ry, two, 1 - x))
        relay = sends.go(wc.at[end], w.at[ry, end, x], xsend.at[0], xrecv.at[0], xx)
        for i, (ref, t, zs, side) in enumerate(own):
            arrivals.append(sends.go(ref, w.at[t, zs, side], wsend.at[i], wrecv.at[i], core))
            fills.append(pltpu.make_async_copy(ref, w.at[t, zs, side], loc.at[1 + i]))
    else:
        fills.append(pltpu.make_async_copy(wfull, w, loc.at[1]))
    for c in fills:
        c.start()
    for part in heads[1:]:
        for c in part:
            c.start()
    sums_o[...] = jnp.zeros_like(sums_o)
    vecs = vec[...]
    out_bias, outer_bias = vecs[0:1], vecs[1:2]
    gain1, gain2, shift1, shift2 = vecs[2:3], vecs[3:4], vecs[4:5], vecs[5:6]
    if with_w:
        relay.wait_recv()
        tail = w.at[ry, end, 1 - x]
        onward = remote(tail, tail, wsend.at[4], wrecv.at[4], core)
        onward.start()
        arrivals.append(onward)
    for c in fills:
        c.wait()
    for c in arrivals:
        c.wait_recv()
    for t in range(4):
        wt_s[t] = jnp.transpose(w[t, :, :, :, 2 * FQ:].reshape(D, PK - 2 * FQ))
    bias_in = [wt_s[t, QW:QW + 16].astype(f32)[0:1] for t in range(4)]
    w_in = lambda t: w[t, :, :, :, 0:FQ].reshape(D, FQ)
    w_ou = lambda t: w[t, :, :, :, FQ:2 * FQ].reshape(D, FQ)

    def add_sum(i, rows):
        sums_o[i:i + 1] += jnp.sum(rows, axis=0, keepdims=True)

    def block(b, _):
        for i in range(NR):
            @pl.when(b == i)
            def _():
                for c in heads[i]:
                    c.wait_recv()
        rows = aligned(b, RB)
        start = inp[rows].astype(f32) + te[...].astype(f32)
        attn = out_bias
        for m in range(4):
            attn = attn + mm(mixr[m, :, rows], wt_s[ranks[m], :QW], TN)
        hidden, normed1, inv1 = layer_norm(start + attn, gain1, shift1)
        low = hidden.astype(bf)
        ht[:, rows] = low.T
        mlp = outer_bias
        for t in range(4):
            u = mm(low, w_in(t)) + bias_in[t]
            value, slope = gelu_parts(u)
            value = value.astype(bf)
            act[t, rows] = value
            slope_s[t] = slope.astype(bf)
            mlp = mlp + mm(value, w_ou(t), NT)
        final, normed2, inv2 = layer_norm(hidden + mlp, gain2, shift2)
        block_out[rows] = final.astype(bf)
        e = cot[rows].astype(f32)
        add_sum(0, e * normed2)
        add_sum(1, e)
        grad2 = norm_back(e, normed2, inv2, gain2)
        gm = grad2.astype(bf)
        gmt[:, rows] = gm.T
        add_sum(2, gm.astype(f32))
        gin = grad2
        for t in range(4):
            g = (mm(gm, w_ou(t)) * slope_s[t].astype(f32)).astype(bf)
            gp[t, rows] = g
            add_sum(6 + t, g.astype(f32))
            gin = gin + mm(g, w_in(t), NT)
        add_sum(3, gin * normed1)
        add_sum(4, gin)
        grad1 = norm_back(gin, normed1, inv1, gain1)
        grad1_o[rows] = grad1
        ga = grad1.astype(bf)
        gat_rows = ga.T
        gat[:, rows] = gat_rows
        add_sum(5, ga.astype(f32))
        for m in (3, 2, 1):
            gmix[m, :, rows] = mm(wt_s[ranks[m], :QW], gat_rows).astype(bf)
            heads_out(b, m).start()
        dots[0, :, rows] = mm(wt_s[r, :QW], gat_rows).astype(bf)
        return 0

    lax.fori_loop(0, NR, block, 0)

    if with_w:
        onward.wait_send()

    def grads(t, m):
        return (lambda: mm(ht[...], gp[t]), lambda: mm(gmt[...], act[t]), lambda: mm(gat[...], mixr[m], NT))

    cols = (slice(0, FQ), slice(FQ, 2 * FQ), slice(2 * FQ, 2 * FQ + QW))
    blank = jnp.zeros((4, 2, 96, PK - 2 * FQ - QW), bf)
    cut = lambda g: g.reshape(4, 2, 96, g.shape[1])

    def handing(q):
        return remote(w.at[q], both.at[q], gsend.at[q], grecv.at[q], core)

    for q in (1, 0):
        for c, g in zip(cols, grads(ranks[2 * q + 1], 2 * q + 1)):
            w[q, :, :, :, c] = cut(g().astype(bf))
        w[q, :, :, :, 2 * FQ + QW:] = blank
        handing(q).start()
    saves = []
    for q in (1, 0):
        mine = grads(ranks[2 * q], 2 * q)
        handing(q).wait_recv()
        for c, g in zip(cols, mine):
            both[q, :, :, :, c] = (both[q, :, :, :, c].astype(f32) + cut(g())).astype(bf)
        for n, side in ((0, x), (1, 1 - x)):
            to = ((p00, p01), (p10, p11))[q][n]
            saves.append(pltpu.make_async_copy(both.at[q, :, side], to, loc.at[6 + 2 * q + n]))
            saves[-1].start()
    for b in range(NR):
        for m in (1, 2, 3):
            heads_out(b, m).wait()
        for c in heads[b]:
            c.wait_send()
    saves.append(pltpu.make_async_copy(dots, dots_hbm, loc.at[10]))
    saves[-1].start()
    for c in saves:
        c.wait()
    for q in range(2):
        handing(q).wait_send()
    sends.drain()


def middle(weights, mix, inp, te, cot, vec):
    sd = jax.ShapeDtypeStruct
    dma = pltpu.SemaphoreType.DMA
    with_w = len(weights) > 1
    vm = pltpu.VMEM
    tokens = (D, ROWS)
    extra = [dma((1,)), dma((1,)), dma((5,)), dma((5,))] if with_w else []
    return pl.pallas_call(
        functools.partial(middle_kernel, with_w),
        out_shape=(sd((ROWS, D), bf), sd((ROWS, D), f32), sd((4, QW, ROWS), bf),
                   *([sd((4, 96, PK), bf)] * 4), sd((16, D), f32)),
        in_specs=[HB] * len(weights) + [HB] + [VM] * 4, out_specs=(VM, VM, HB, HB, HB, HB, HB, VM),
        scratch_shapes=[vm((4, 4, 2, 96, PK), bf), vm((4, PK - 2 * FQ, D), bf), vm((4, QW, ROWS), bf),
                        vm((4, QW, ROWS), bf), vm((4, QW, ROWS), bf), vm((4, QW, ROWS), bf),
                        vm((2, 4, 2, 96, PK), bf), vm(tokens, bf), vm(tokens, bf), vm(tokens, bf),
                        vm((4, ROWS, FQ), bf), vm((4, ROWS, FQ), bf), vm((4, RB, FQ), bf),
                        dma((11,)), dma((NR, 4)), dma((NR, 4)), dma((NR, 4)), dma((NR, 4)), dma((2,)), dma((2,))] + extra,
        compiler_params=pltpu.CompilerParams(collective_id=2, has_side_effects=True, vmem_limit_bytes=63 << 20),
        cost_estimate=pl.CostEstimate(flops=33_000_000_000, bytes_accessed=50_000_000, transcendentals=9_000_000),
        name="middle",
    )(*weights, mix, inp, te, cot, vec)


def final_kernel(with_w, *refs):
    if with_w:
        (x_hbm, w_hbm, dqt_hbm, dkv_hbm, g1_hbm, m0_hbm, m1_hbm, m2_hbm, m3_hbm, small, out, pair, qo, mo, tot,
         x_s, w_s, wr_s, dqt, dkv, grad1, part, crv, ysd, yrv, m0, m1, m2, m3, zsm, zrm, dwq, xrq, zsq, zrq,
         prv, psd, prs, loc, csend, crecv, ysend, yrecv, xsend, xrecv, zsend, zrecv) = refs
    else:
        (x_hbm, w_hbm, dqt_hbm, dkv_hbm, g1_hbm, out, pair, dw,
         x_s, w_s, wr_s, dqt, dkv, grad1, part, crv, ysd, yrv, loc, csend, crecv, ysend, yrecv) = refs
    pulls = [(w_hbm, w_s), (dqt_hbm, dqt), (dkv_hbm, dkv)]
    pulls += [(m0_hbm, m0), (m1_hbm, m1), (m2_hbm, m2), (m3_hbm, m3)] if with_w else []
    pulls += [(x_hbm, x_s), (g1_hbm, grad1)]
    loads = [pltpu.make_async_copy(a, b, loc.at[n]) for n, (a, b) in enumerate(pulls)]
    for c in loads:
        c.start()
    r = lax.axis_index("tensor")
    d = lax.axis_index("dp")
    rc, ry = flip1(r), lax.rem(r + 2, 4)
    rd = 3 - r
    core, yy = {"tensor": rc}, {"tensor": ry}
    targets = [core, yy]
    if with_w:
        z, x = d // 2, lax.rem(d, 2)
        xo = 1 - x
        zs = [lax.rem(z + k, 4) for k in range(4)]
        xx = {"dp": flip1(d)}
        zdev = [{"dp": zs[k] * 2 + x} for k in range(4)]
        targets += [xx] + zdev[1:]
    meet(targets)
    sends = Sends()
    go = sends.go
    wait = lambda *which: [loads[n].wait() for n in which]
    rows = [pl.ds(i * CROWS, CROWS) for i in range(CH)]
    if with_w:
        wait(3, 4, 5, 6)
        zm = []
        for k in (1, 2, 3, 0):
            at = zs[k]
            zsm[k] = ((m0[at].astype(f32) + m1[at].astype(f32)) + (m2[at].astype(f32) + m3[at].astype(f32))).astype(bf)
            if k:
                zm.append(go(zsm.at[k], zrm.at[k - 1], zsend.at[1, k - 1], zrecv.at[1, k - 1], zdev[k]))
    wait(0, 1, 2)
    w = w_s[...].reshape(D, 3 * QW)
    for h in range(HN):
        for c in (1, 2):
            wr_s[:, h * 128 + (c - 1) * HD:h * 128 + c * HD] = w[:, c * QW + h * HD:c * QW + (h + 1) * HD]
    wqs = w[:, :QW]

    def project_back(t, i):
        at = pl.ds(pl.multiple_of(t * ROWS + i * CROWS, CROWS), CROWS)
        part[t, rows[i]] = (mm(dqt[:, at], wqs, (((0,), (1,)), ((), ()))) + mm(dkv[at], wr_s[...], NT)).astype(bf)

    first, second, third = [], [], []
    for i in range(CH):
        project_back(rd, i)
        second.append(go(part.at[rd, rows[i]], crv.at[1, rows[i]], csend.at[1, i], crecv.at[1, i], core))
        project_back(ry, i)
        if i:
            second[i - 1].wait_recv()
            prev = rows[i - 1]
            ysd[prev] = (part[ry, prev].astype(f32) + crv[1, prev].astype(f32)).astype(bf)
            third.append(go(ysd.at[prev], yrv.at[prev], ysend.at[i - 1], yrecv.at[i - 1], yy))
    prev = rows[CH - 1]
    second[CH - 1].wait_recv()
    ysd[prev] = (part[ry, prev].astype(f32) + crv[1, prev].astype(f32)).astype(bf)
    third.append(go(ysd.at[prev], yrv.at[prev], ysend.at[CH - 1], yrecv.at[CH - 1], yy))

    wait(len(loads) - 2)
    whole = x_s[...].reshape(SEQ, D)
    aq = mm(dqt[...], whole)
    akv = mm(dkv[...], whole, TN)
    blocks = [aq]
    for c in (0, 1):
        blocks += [akv[h * 128 + c * HD:h * 128 + (c + 1) * HD] for h in range(HN)]
    dwt = jnp.concatenate(blocks, 0).T.astype(bf)
    sum_q = jnp.sum(dqt[...].astype(f32), axis=1, keepdims=True)
    sum_q = jnp.transpose(jnp.broadcast_to(sum_q, (QW, 8)))
    sum_kv = jnp.sum(dkv[...].astype(f32), axis=0, keepdims=True)
    sum_v = jnp.concatenate([sum_kv[:, h * 128 + HD:(h + 1) * 128] for h in range(HN)], 1)
    pairs = jnp.concatenate([sum_q[0:1], sum_v, jnp.zeros((6, QW), f32)], 0)
    if with_w:
        dwq[...] = dwt.reshape(dwq.shape)
        xq = go(dwq.at[:, xo], xrq, xsend.at[0], xrecv.at[0], xx)
        prs[...] = pairs
        px = go(prs, prv, xsend.at[1], xrecv.at[1], xx)
    for i in range(CH):
        project_back(rc, i)
        first.append(go(part.at[rc, rows[i]], crv.at[0, rows[i]], csend.at[0, i], crecv.at[0, i], core))
        project_back(r, i)
    if with_w:
        tot[...] = jnp.sum(small[...], axis=0)
        px.wait_recv()
        psd[z] = prs[...] + prv[...]
        zp = [go(psd.at[z], psd.at[z], zsend.at[2, k - 1], zrecv.at[2, k - 1], zdev[k]) for k in (1, 2, 3)]
        xq.wait_recv()
        for k in range(4):
            zsq[k] = (dwq[zs[k], x].astype(f32) + xrq[zs[k]].astype(f32)).astype(bf)
        zq = [go(zsq.at[k], zrq.at[k - 1], zsend.at[0, k - 1], zrecv.at[0, k - 1], zdev[k]) for k in (1, 2, 3)]
    else:
        dw[...] = dwt
        pair[...] = pairs
    wait(len(loads) - 1)
    for i in range(CH):
        first[i].wait_recv()
        third[i].wait_recv()
        out[rows[i]] = (part[r, rows[i]].astype(f32) + crv[0, rows[i]].astype(f32)
                        + yrv[rows[i]].astype(f32) + grad1[rows[i]]).astype(bf)
    if with_w:
        for c in zq:
            c.wait_recv()
        whole_q = (zsq[0].astype(f32) + zrq[0].astype(f32)) + (zrq[1].astype(f32) + zrq[2].astype(f32))
        qo[...] = whole_q
        for c in zp:
            c.wait_recv()
        pair[...] = ((psd[0] + psd[1]) + psd[2]) + psd[3]
        for c in zm:
            c.wait_recv()
        mo[...] = (zsm[0].astype(f32) + zrm[0].astype(f32)) + (zrm[1].astype(f32) + zrm[2].astype(f32))
    sends.drain()


def final(whole, w, dqt, dkv, grad1, *more):
    with_w = len(more) > 0
    dma = pltpu.SemaphoreType.DMA
    sd = jax.ShapeDtypeStruct
    vm = pltpu.VMEM
    rows = (ROWS, D)
    like = lambda a: vm(a.shape, a.dtype)
    shapes = [sd(rows, bf), sd((8, QW), f32)]
    args = [whole, w, dqt, dkv, grad1, *more]
    scratch = [like(whole), like(w), vm((D, 2 * QW), bf), like(dqt), like(dkv), like(grad1), vm((4,) + rows, bf),
               vm((2,) + rows, bf), vm(rows, bf), vm(rows, bf)]
    sems = [dma((9,)), dma((2, CH)), dma((2, CH)), dma((CH,)), dma((CH,))]
    if with_w:
        n = w.shape[1]
        shapes += [sd((n, 3 * QW), f32), sd((n, PK), f32), sd(more[4].shape[1:], f32)]
        scratch += [like(m) for m in more[:4]] + [vm((4, n, PK), bf), vm((3, n, PK), bf),
                    vm((4, 2, n, 3 * QW), bf), vm((4, n, 3 * QW), bf), vm((4, n, 3 * QW), bf), vm((3, n, 3 * QW), bf),
                    vm((8, QW), f32), vm((4, 8, QW), f32), vm((8, QW), f32)]
        sems += [dma((2,)), dma((2,)), dma((3, 3)), dma((3, 3))]
    else:
        shapes += [sd((D, 3 * QW), bf)]
    return pl.pallas_call(
        functools.partial(final_kernel, with_w),
        out_shape=shapes,
        in_specs=[HB] * (len(args) - 1) + [VM if with_w else HB], out_specs=[VM] * len(shapes),
        scratch_shapes=scratch + sems,
        compiler_params=pltpu.CompilerParams(
            collective_id=1, has_side_effects=True, vmem_limit_bytes=60 << 20),
        name="final",
    )(*args)


def emit_kernel(rank, *refs):
    sources, outs, kept, sem = refs[:6], refs[6:18], refs[18:24], refs[24]
    loads = [pltpu.make_async_copy(a, b, sem.at[n]) for n, (a, b) in enumerate(zip(sources, kept))]
    for c in loads:
        c.start()
    block_out, input_grad, qkv_o, pair_o, out_o, out_b, inner_o, inner_b, outer_o, outer_b, gain_o, shift_o = outs
    saves = [pltpu.make_async_copy(kept[n], to, sem.at[6 + n]) for n, to in enumerate((block_out, input_grad))]
    for n in range(2):
        loads[n].wait()
        saves[n].start()
    for c in loads[2:]:
        c.wait()
    pair, qkv, share, sums = kept[2:]
    for c in range(3):
        qkv_o[c] = qkv[:, c * QW:(c + 1) * QW]
    pair_o[...] = pair[0:2]
    inner_o[...] = share[:, 0:FQ]
    outer_o[...] = share[:, FQ:2 * FQ]
    out_o[...] = share[:, 2 * FQ:].T[:QW]
    out_b[...] = sums[5]
    inner_b[...] = sums[6 + rank[0]]
    outer_b[...] = sums[2]
    gain_o[...] = jnp.concatenate([sums[3:4], sums[0:1]], 0)
    shift_o[...] = jnp.concatenate([sums[4:5], sums[1:2]], 0)
    for c in saves:
        c.wait()


def emit(rank, *arrays):
    sd = jax.ShapeDtypeStruct
    n = arrays[4].shape[0]
    rows = sd((ROWS, D), bf)
    vec = sd((D,), f32)
    shapes = (rows, rows, sd((3, n, QW), f32), sd((2, QW), f32), sd((QW, n), f32), vec, sd((n, FQ), f32), vec,
              sd((n, FQ), f32), vec, sd((2, D), f32), sd((2, D), f32))
    return pl.pallas_call(
        emit_kernel, out_shape=shapes, in_specs=[SM] + [HB] * 6, out_specs=(HB, HB) + (VM,) * 10,
        scratch_shapes=[pltpu.VMEM(a.shape, a.dtype) for a in arrays] + [pltpu.SemaphoreType.DMA((8,))],
        compiler_params=pltpu.CompilerParams(vmem_limit_bytes=60 << 20),
        name="emit",
    )(rank.reshape(1), *arrays)


def add_low(a, b):
    return (a.astype(f32) + b.astype(f32)).astype(bf)


def on_device(
    ring, input_rows, time_embed, parents, qkv_weight, qv_bias, out_weight, out_bias, inner_weight,
    inner_bias, outer_weight, outer_bias, norm_gain, norm_shift, cotangent,
):
    rank = lax.axis_index("tensor")
    dpos = lax.axis_index("dp")
    part = qkv_weight.shape[0]
    own_ring = ring == 8
    order = jnp.stack([rank, rank ^ 1, rank ^ 2, rank ^ 3]).astype(jnp.int32)

    bias = qv_bias.astype(f32).reshape(1, 2 * QW)
    if own_ring:
        whole, w_all, gz, gx = gather_start(
            input_rows, time_embed, jnp.transpose(qkv_weight, (1, 0, 2)), inner_weight, outer_weight.T, out_weight,
            inner_bias[None])
        weights = [gz, gx, partner(gz, 2), partner(gx[:2], 2)]
    else:
        whole = gather_start(input_rows, time_embed)[0]
        w_all = lax.all_gather(qkv_weight.reshape(part, 3 * QW), "dp", axis=0, tiled=True).reshape(8, 96, 3 * QW)
        bias_part = lax.dynamic_slice_in_dim(inner_bias, dpos * part, part, 0)
        packed = jnp.concatenate([inner_weight, outer_weight.T, out_weight.T, bias_part[:, None],
                                  jnp.zeros((part, PK - 2 * FQ - QW - 1), bf)], axis=1)
        packed = lax.all_gather(packed, "dp", axis=0, tiled=True)
        weights = [lax.all_gather(packed, "tensor", axis=0, tiled=False).reshape(4, 4, 2, 96, PK)]

    qt, kv, kt, ot, mix, lse, pairs = attn_fwd(parents[0], order, whole, w_all, bias)
    vec = jnp.concatenate(
        [out_bias[None], outer_bias[None], norm_gain, norm_shift, jnp.zeros((2, D), bf)], axis=0).astype(f32)
    block_out, grad1, dots, *parts, sums = middle(weights, mix, input_rows, time_embed, cotangent, vec)
    sums = lax.all_gather(sums, ("dp", "tensor"), axis=0, tiled=False)
    if own_ring:
        diagonal = [(i * 4 + j, (i ^ 1) * 4 + (j ^ 2)) for i in range(8) for j in range(4)]
        parts = [parts[0], across_x(parts[1]), partner(parts[2], 2), lax.ppermute(parts[3], ("dp", "tensor"), diagonal)]
    else:
        far = [partner(parts[2], 2), partner(parts[3], 2)]
    dqt, dkv = attn_bwd((0, 1, 2), pairs, order, qt, kv, kt, dots, ot, lse)
    if own_ring:
        input_grad, pair, qkv_share, share, sums = final(whole, w_all, dqt, dkv, grad1, *parts, sums)
        (block_out, input_grad, qkv_share, pair, out_share, out_sum, inner_share, inner_sum, outer_share, outer_sum,
         gains, shifts) = emit(rank, block_out, input_grad, pair, qkv_share, share, sums)
        return (block_out, input_grad, jnp.transpose(qkv_share, (1, 0, 2)), pair, out_share, out_sum,
                inner_share, inner_sum, outer_share.T, outer_sum, gains, shifts)
    else:
        input_grad, pair, dwq = final(whole, w_all, dqt, dkv, grad1)
        own, other = add_low(parts[0], far[0]), add_low(parts[1], far[1])
        even = dpos % 2 == 0
        mine = jnp.stack([jnp.where(even, own, other), jnp.where(even, other, own)], axis=1).reshape(D, PK)
        share = lax.psum_scatter(mine, "dp", scatter_dimension=0, tiled=True).astype(f32)
        qkv_share = lax.psum_scatter(dwq, "dp", scatter_dimension=0, tiled=True).astype(f32).reshape(part, 3, QW)
        pair = lax.psum(pair, "dp")
        sums = jnp.sum(sums, axis=0)
    return (
        block_out,
        input_grad,
        qkv_share,
        pair[:2],
        share[:, 2 * FQ:2 * FQ + QW].T,
        sums[5],
        share[:, :FQ],
        lax.dynamic_index_in_dim(sums[6:10], rank, 0, keepdims=False),
        share[:, FQ:2 * FQ].T,
        sums[2],
        jnp.stack([sums[3], sums[0]]),
        jnp.stack([sums[4], sums[1]]),
    )


def solution(mesh):
    both = P(("dp", "tensor"), None)
    return jax.shard_map(
        functools.partial(on_device, mesh.shape["dp"]),
        mesh=mesh,
        in_specs=(
            both, P("dp", None), P("dp", None), P("dp", None, "tensor"), P(None, "tensor"),
            P("tensor", "dp"), P(), P("dp", "tensor"), P("tensor"), P("tensor", "dp"), P(), P(), P(), both,
        ),
        out_specs=(
            both, both, P("dp", None, "tensor"), P(None, "tensor"), P("tensor", "dp"), P(),
            P("dp", "tensor"), P("tensor"), P("tensor", "dp"), P(), P(), P(),
        ),
        check_vma=False,
    )
```

time: 680 us -> 323 us (0.47); the launches traced: 682 us -> 318 us
  Pallas kernels: 136 us -> 280 us
  waiting for transfers between devices: 154 us -> 10.9 us
  blocking collectives: 141 us -> 0 us
  matrix products: 109 us -> 0 us
  local copies, waits for them, and re-layouts: 75.2 us -> 4.02 us
  other arithmetic: 42.8 us -> 1.2 us
    pallas_call x2 -> x6, Pallas kernels: 136 us -> 280 us  [the longest x1 72.1 us: middle(): pl.pallas_call(functools.partial(middle_kernel, with_w), out_shape=(sd((R...]
    dot_general x32 -> x0, matrix products: 109 us -> none  [the longest x4 15.3 us: on_device(): mlp = mlp + jnp.einsum('tf,df->td', acts[t], outer_t[t], **wide)]
    psum x1 -> x0, blocking collectives: 89.9 us -> none  [on_device(): lax.psum(jnp.concatenate([pair, jnp.stack(inner_sums), jnp.stack([out_bia...]
    ppermute x10 -> x3, waiting for transfers between devices: 76.5 us -> 3.59 us  [partner(): return lax.ppermute(x, 'tensor', [(i, i ^ mask) for i in range(4)])]
    all_gather x2 -> x1, waiting for transfers between devices: 59.5 us -> 7.27 us  [on_device(): sums = lax.all_gather(sums, ('dp', 'tensor'), axis=0, tiled=False)]
    all_gather x2 -> x0, blocking collectives: 51.2 us -> none  [the longest x1 33.4 us: on_device(): lax.all_gather(qkv_weight.reshape(part, 3 * QW), 'dp', axis=0, tiled=True)]
    unnamed x154 -> x16, local copies, waits for them, and re-layouts: 39 us -> 0.92 us
    unnamed x6 -> x1, waiting for transfers between devices: 17.8 us -> 0.02 us
  transfers between devices with their start and end apart: 15 -> 6, of which waited for: 5 -> 2; matrix products, arithmetic and copies ran while one was open for 18% -> 1% of each run, Pallas kernels for 20% -> 33%
where the time goes in v2:
time: 323 us; the launch traced here: 318 us
  Pallas kernels  280 us (87%)
  between operations  14.6 us (5%)
  waiting for transfers between devices  10.9 us (3%)
  starting transfers between devices  7.7 us (2%)
  local copies, waits for them, and re-layouts  4.02 us (1%)
    pallas_call x1, Pallas kernels, middle(): pl.pallas_call(functools.partial(middle_kernel, with_w), out_shape=(sd((R...  72.1 us
    pallas_call x1, Pallas kernels, attn_bwd(): pl.pallas_call(functools.partial(bwd_kernel, heads), out_shape=(sd((n * H...  59.9 us
    pallas_call x1, Pallas kernels, gather_start(): pl.pallas_call(functools.partial(gather_kernel, with_w), out_shape=shapes...  50.6 us
    pallas_call x1, Pallas kernels, final(): pl.pallas_call(functools.partial(final_kernel, with_w), out_shape=shapes,...  48.7 us
    pallas_call x1, Pallas kernels, attn_fwd(): pl.pallas_call(fwd_kernel, out_shape=(sd((n, S), bf), sd((S, 2 * n), bf),...  44.2 us
    all_gather x1, waiting for transfers between devices, on_device(): sums = lax.all_gather(sums, ('dp', 'tensor'), axis=0, tiled=False)  7.27 us
  transfers between devices with their start and end apart: 6, of which 2 were waited for; matrix products, arithmetic and copies ran while one was open for 1% of the time, Pallas kernels for 33%

profile of v2, /device:TPU:0, one launch (start us, length us, event | category | flops | bytes accessed | tf_op | source)
XLA Modules:
  0.0 318.0 jit_solution(14868397681404615862)
XLA Ops:
  7.2 0.0 all-gather.3.cloned.1.call-start
  7.2 1.3 broadcast_in_dim.12.refs_6_
  8.5 0.0 copy-start.6
  8.5 50.6 %gather_start.1 = (bf16[4,1024,768]{2,1,0:T(8,128)(2,1)}, bf16[8,96,576]{2,1,0:T(8,128)(2,1)}, bf16[4,96,1792]{2,1,0:T(8,128)(2,1)}, bf16[4,96,1792]{2,1,0:T(8,128)(2,1)}) custom-call(bf16[1024,768]{1,0:T(8,128)(2,1)} %refs_5_.3, bf16[1,768]{1,0:T(2,128)(2,1)} %refs_6_.1, bf16[3,96,192]{2,1,0:T(8,128)(2,1)} %bitcast.11, bf16[96,768]{1,0:T(8,128)(2,1)} %refs_3_.1, ...), custom_call_target="tpu_custom_call" | custom-call | tf_op jit(solution)/shard_map/gather_start/pallas_call | solution.py:519
  59.1 1.1 slice.3
  60.3 1.6 collective-permute-start.1
  61.9 0.5 collective-permute-start
  62.4 0.0 copy-done.6
  62.4 0.6 reshape.36.b_ref
  63.0 0.6 pad_add_fusion.tab
  63.6 0.0 copy-start.4
  63.6 0.0 copy-start.5
  63.6 0.0 copy-start.2
  63.6 0.0 copy-start.3
  63.6 44.2 %tree_attention.1 = (bf16[192,4096]{1,0:T(8,128)(2,1)}, bf16[4096,384]{1,0:T(8,128)(2,1)}, bf16[192,4096]{1,0:T(8,128)(2,1)}, f32[192,4096]{1,0:T(8,128)}, bf16[...) custom-call(s32[13]{0:T(128)} %bitcast.15, s32[4]{0:T(128)} %pad_add_fusion.tab, ...), custom_call_target="tpu_custom_call" | custom-call | flops 40000000000 | bytes 12000000 | tf_op jit(solution)/shard_map/tree_attention/pallas_call | solution.py:174
  107.8 0.0 copy-done.4
  107.8 0.0 copy-done.5
  107.9 0.0 copy-done.2
  107.9 0.0 copy-done.3
  107.9 0.6 convert_element_type.4.refs_8_
  108.5 0.0 collective-permute-done.1.refs_3_
  108.5 0.0 copy-start.7
  108.5 0.0 collective-permute-done.refs_2_
  108.5 0.9 copy-done.7
  109.4 72.1 %middle.1 = (bf16[1024,768]{1,0:T(8,128)(2,1)}, f32[1024,768]{1,0:T(8,128)}, bf16[4,192,1024]{2,1,0:T(8,128)(2,1)}, bf16[4,96,1792]{2,1,0:T(8,128)(2,1)}, bf16[4...) custom-call(bf16[4,96,1792]{2,1,0:T(8,128)(2,1)} %get-tuple-element.50., ...), custom_call_target="tpu_custom_call" | custom-call | flops 32999999488 | bytes 50000000 | tf_op jit(solution)/shard_map/middle/pallas_call | solution.py:707
  181.6 0.0 all-gather.3.cloned.1.call-update
  181.6 4.0 %collective-permute-start.2 = (bf16[4,96,1792]{2,1,0:T(8,128)(2,1)}, bf16[4,96,1792]{2,1,0:T(8,128)(2,1)S(1)}, u32[]{:S(2)}, u32[]{:S(2)}) collective-permute-start(bf16[4,96,1792]{2,1,0:T(8,128)(2,1)} %get-tuple-element.67), channel_id=1, source_target_pairs={{0,4},{4,0},{8,12},{12,8},{16,20},{20,16},{24,28},{28,24},{1,5},{5... | collective-permute-start | bytes 4128776 | tf_op jit(solution)/shard_map/ppermute | solution.py:333
  185.6 0.5 collective-permute-start.3
  186.1 1.0 collective-permute-start.4
  187.2 59.9 %tree_attention_grad.1 = (bf16[192,4096]{1,0:T(8,128)(2,1)}, bf16[4096,384]{1,0:T(8,128)(2,1)}) custom-call(s32[3,192]{1,0:T(4,128)} %get-tuple-element.56.pairs, s32[4]{0:T(128)} %pad_add_fusion.tab, bf16[192,4096]{1,0:T(8,128)(2,1)} %get-tuple-element.57.qt_hbm, bf16[4096,384]{1,0:T(8,128)(2,1)} %get-tuple-element.58.kv_hbm, ...), custom_call_target="tpu_custom_call" | custom-call | flops 60000002048 | bytes 24000000 | tf_op jit(solution)/shard_map/tree_attention_grad/pallas_call | solution.py:278
  247.0 0.0 collective-permute-done.2.refs_6_
  247.0 0.0 copy-start
  247.0 3.6 %collective-permute-done.3.refs_7_ = bf16[4,96,1792]{2,1,0:T(8,128)(2,1)S(1)} collective-permute-done((bf16[4,96,1792]{2,1,0:T(8,128)(2,1)}, bf16[4,96,1792]{2,1,0:T(8,128)(2,1)S(1)}, u32[]{:S(2)}, u32[]{:S(2)}) %collective-permute-start.3) | collective-permute-done | bytes 1376288 | tf_op jit(solution)/shard_map/ppermute | solution.py:329
  250.6 0.0 copy-start.1
  250.6 0.0 collective-permute-done.4.refs_8_
  250.6 7.3 %all-gather.3.cloned.1.call-done = f32[512,768]{1,0:T(8,128)} async-done(((f32[16,768]{1,0:T(8,128)}), f32[512,768]{1,0:T(8,128)}) %all-gather.3.cloned.1.call-update) | async-done | bytes 1572880 | tf_op jit(solution)/shard_map/all_gather | solution.py:951
  257.9 0.0 copy-done
  257.9 0.0 copy-done.1
  257.9 48.7 %final.1 = (bf16[1024,768]{1,0:T(8,128)(2,1)}, f32[8,192]{1,0:T(8,128)}, f32[96,576]{1,0:T(8,128)}, f32[96,1792]{1,0:T(8,128)}, f32[16,768]{1,0:T(8,128)}) custom-call(bf16[4,1024,768]{2,1,0:T(8,128)(2,1)} %get-tuple-element.52.x_hbm.refs_0_, bf16[8,96,576]{2,1,0:T(8,128)(2,1)} %get-tuple-element.53.w_hbm.refs_1_, ...), custom_call_target="tpu_custom_call" | custom-call | tf_op jit(solution)/shard_map/final/pallas_call | solution.py:864
  306.6 4.1 %emit.1 = (bf16[1024,768]{1,0:T(8,128)(2,1)}, bf16[1024,768]{1,0:T(8,128)(2,1)}, f32[3,96,192]{2,1,0:T(8,128)}, f32[2,192]{1,0:T(2,128)}, f32[192,96]{1,0:T(8,12...) custom-call(s32[1]{0:T(128)} %bitcast.rank, ...), custom_call_target="tpu_custom_call" | custom-call | tf_op jit(solution)/shard_map/emit/pallas_call | solution.py:910
  (4 shorter events, 0.1 us)
Async XLA Ops:
  7.2 250.7 %all-gather.3.cloned.1.call-start = ((), (), s32[]{:S(2)}) async-start(), calls=%async_computation | async-start | bytes 1622016 | tf_op jit(solution)/shard_map/all_gather | solution.py:951
  8.5 53.9 %copy-start.6 = (bf16[2,192]{1,0:T(2,128)(2,1)S(1)}, bf16[2,192]{1,0:T(2,128)(2,1)}, u32[]{:S(2)}) copy-start(bf16[2,192]{1,0:T(2,128)(2,1)} %param.18) | copy-start | bytes 2308
  60.3 48.3 %collective-permute-start.1 = (bf16[2,96,1792]{2,1,0:T(8,128)(2,1)S(1)}, bf16[2,96,1792]{2,1,0:T(8,128)(2,1)S(1)}, u32[]{:S(2)}, u32[]{:S(2)}) collective-permute-start(bf16[2,96,1792]{2,1,0:T(8,128)(2,1)S(1)} %slice.3), channel_id=1, source_target_pairs={{0,2},{1,3},{2,0},{3,1},{4,6},{5,7},{6,4},{7,5},{8,10},{9,11},{10,... | collective-permute-start | bytes 2064392 | tf_op jit(solution)/shard_map/ppermute | solution.py:329
  61.9 46.7 %collective-permute-start = (bf16[4,96,1792]{2,1,0:T(8,128)(2,1)}, bf16[4,96,1792]{2,1,0:T(8,128)(2,1)}, u32[]{:S(2)}, u32[]{:S(2)}) collective-permute-start(bf16[4,96,1792]{2,1,0:T(8,128)(2,1)} %get-tuple-element.50.refs_0_), channel_id=1, source_target_pairs={{0,2},{1,3},{2,0},{3,1},{4,6},{5,7},{6,4},{7,5},{8,10},{9,11},{10,... | collective-permute-start | bytes 4128776 | tf_op jit(solution)/shard_map/ppermute | solution.py:329
  63.6 44.2 %copy-start.4 = (bf16[768]{0:T(1024)(128)(2,1)S(1)}, bf16[768]{0:T(1024)(128)(2,1)}, u32[]{:S(2)}) copy-start(bf16[768]{0:T(1024)(128)(2,1)} %param.20) | copy-start | bytes 4612
  63.6 44.2 %copy-start.5 = (bf16[768]{0:T(1024)(128)(2,1)S(1)}, bf16[768]{0:T(1024)(128)(2,1)}, u32[]{:S(2)}) copy-start(bf16[768]{0:T(1024)(128)(2,1)} %param.24) | copy-start | bytes 4612
  63.6 44.3 %copy-start.2 = (bf16[2,768]{1,0:T(2,128)(2,1)S(1)}, bf16[2,768]{1,0:T(2,128)(2,1)}, u32[]{:S(2)}) copy-start(bf16[2,768]{1,0:T(2,128)(2,1)} %param.25) | copy-start | bytes 9220
  63.6 44.3 %copy-start.3 = (bf16[2,768]{1,0:T(2,128)(2,1)S(1)}, bf16[2,768]{1,0:T(2,128)(2,1)}, u32[]{:S(2)}) copy-start(bf16[2,768]{1,0:T(2,128)(2,1)} %param.26) | copy-start | bytes 9220
  108.5 0.9 copy-start.7
  181.6 65.4 %collective-permute-start.2 = (bf16[4,96,1792]{2,1,0:T(8,128)(2,1)}, bf16[4,96,1792]{2,1,0:T(8,128)(2,1)S(1)}, u32[]{:S(2)}, u32[]{:S(2)}) collective-permute-start(bf16[4,96,1792]{2,1,0:T(8,128)(2,1)} %get-tuple-element.67), channel_id=1, source_target_pairs={{0,4},{4,0},{8,12},{12,8},{16,20},{20,16},{24,28},{28,24},{1,5},{5... | collective-permute-start | bytes 4128776 | tf_op jit(solution)/shard_map/ppermute | solution.py:333
  185.6 65.0 %collective-permute-start.3 = (bf16[4,96,1792]{2,1,0:T(8,128)(2,1)}, bf16[4,96,1792]{2,1,0:T(8,128)(2,1)S(1)}, u32[]{:S(2)}, u32[]{:S(2)}) collective-permute-start(bf16[4,96,1792]{2,1,0:T(8,128)(2,1)} %get-tuple-element.68), channel_id=1, source_target_pairs={{0,2},{1,3},{2,0},{3,1},{4,6},{5,7},{6,4},{7,5},{8,10},{9,11},{10,... | collective-permute-start | bytes 4128776 | tf_op jit(solution)/shard_map/ppermute | solution.py:329
  186.1 64.5 %collective-permute-start.4 = (bf16[4,96,1792]{2,1,0:T(8,128)(2,1)}, bf16[4,96,1792]{2,1,0:T(8,128)(2,1)}, u32[]{:S(2)}, u32[]{:S(2)}) collective-permute-start(bf16[4,96,1792]{2,1,0:T(8,128)(2,1)} %get-tuple-element.69), channel_id=1, source_target_pairs={{0,6},{1,7},{2,4},{3,5},{4,2},{5,3},{6,0},{7,1},{8,14},{9,15},{10,... | collective-permute-start | bytes 4128776 | tf_op jit(solution)/shard_map/ppermute | solution.py:954
  247.0 10.9 %copy-start = (bf16[4,96,1792]{2,1,0:T(8,128)(2,1)}, bf16[4,96,1792]{2,1,0:T(8,128)(2,1)S(1)}, u32[]{:S(2)}) copy-start(bf16[4,96,1792]{2,1,0:T(8,128)(2,1)S(1)} %collective-permute-done.2.refs_6_) | copy-start | bytes 4128772
  250.6 7.3 %copy-start.1 = (bf16[4,96,1792]{2,1,0:T(8,128)(2,1)}, bf16[4,96,1792]{2,1,0:T(8,128)(2,1)S(1)}, u32[]{:S(2)}) copy-start(bf16[4,96,1792]{2,1,0:T(8,128)(2,1)S(1)} %collective-permute-done.3.refs_7_) | copy-start | bytes 4128772
Sparse Core Ops, SparseCore 0:
  181.7 76.1 all-gather.2
